TPU v7x, 32 devices: a whole 2x2x4 slice. The times are simulated.
32 devices in a mesh: groups: 2 (over x), domain: 16 (over z, y, core).
Axes of the slice: x: 2, y: 2, z: 4, core: 2. Of those that a mesh axis runs over, the one named last changes fastest.
Arguments:
- patches: bfloat16 [512, 125, 256], P(('groups', 'domain')), parts along dimension 0, may hold values from -6 to 6
- destination: int32 [512], P(('groups', 'domain')), parts along dimension 0, may hold values from 0 to 15, as said below
- cotangent: bfloat16 [1024, 4, 512], P(('groups', 'domain')), parts along dimension 0, may hold values from -16 to 16
- conv_weight: bfloat16 [256, 27, 64], replicated, may hold values from -0.21875 to 0.21875
- conv_bias: float32 [64], replicated, may hold values from -3 to 3
- head_weight: float32 [64, 4], replicated, may hold values from -0.75 to 0.75
Outputs:
- grad_conv: float32 [512, 27, 64], P(('groups', 'domain')), parts along dimension 0
- grad_bias: float32 [128], P('groups'), parts along dimension 0
- grad_head: float32 [128, 4], P('groups'), parts along dimension 0
There are 2 independent parts, one for each index of `groups`. A program takes and returns all parts, laid end to end along the dimension named above; an argument that names none is the same for every part. Nothing has to cross between parts.
Inputs may be any that keep to these rules, and one draw needn't show every extreme that they name: `destination`: each trainer receives at most 32 patches and some trainer exactly 32; one owner sends at most 2 patch to one trainer and some pair reaches it; the patches of one trainer come from the owners as evenly as their number allows.
All inputs are finite; a program needn't handle non-finite values.
Results may differ from a plain program's by a relative error of at most 0.0029.
Values may be sent and summed in bfloat16 or wider, within the bound.
No kernel may reach another device: no remote copies, remote signals or barrier semaphores. Data moves between devices by JAX's collectives and lax.ppermute only.
A program may use at most 64 MiB of HBM per device.

v0:
```python
import jax
import jax.numpy as jnp
import numpy as np
from jax import lax
from jax.sharding import PartitionSpec as P

C_IN = 256
C_OUT = 64
FIELDS = 4
TAPS = 27
PS = 4
PAD = 5
FINE = 512


def shift_plan():
    layout_plan = []
    for first_shift in (0, 1):
        for second_shift in (0, 1):
            for third_shift in (0, 1):
                per_axis = []
                for shift_bit in (first_shift, second_shift, third_shift):
                    per_axis.append([(1, 0)] if shift_bit == 1 else [(0, 1), (1, 2)])
                parity_ids = []
                tap_ids = []
                for first_pair in per_axis[0]:
                    for second_pair in per_axis[1]:
                        for third_pair in per_axis[2]:
                            parity_ids.append(
                                first_pair[0] * 4 + second_pair[0] * 2 + third_pair[0]
                            )
                            tap_ids.append(first_pair[1] * 9 + second_pair[1] * 3 + third_pair[1])
                layout_plan.append(((first_shift, second_shift, third_shift), parity_ids, tap_ids))
    return layout_plan


def local_terms(work_patches, work_cot, conv_weight, conv_bias, head_weight, layout_plan):
    slot_count = work_patches.shape[0]
    block_size = 8
    block_total = slot_count // block_size
    stacked_weights = [
        jnp.concatenate([conv_weight[:, tap_index, :] for tap_index in tap_ids], axis=1)
        for offsets, parity_ids, tap_ids in layout_plan
    ]
    patch_blocks = work_patches.reshape(block_total, block_size, PAD, PAD, PAD, C_IN)
    cot_blocks = work_cot.reshape(block_total, block_size, FIELDS, FINE)
    rows_here = block_size * PS**3

    def block_terms(running, inputs):
        bias_sum, head_sum = running
        padded_cube, cot_block = inputs
        hidden = jnp.zeros((rows_here, 8, C_OUT), jnp.float32)
        for (offsets, parity_ids, tap_ids), stacked in zip(layout_plan, stacked_weights):
            shifted = padded_cube[
                :,
                offsets[0] : offsets[0] + PS,
                offsets[1] : offsets[1] + PS,
                offsets[2] : offsets[2] + PS,
                :,
            ].reshape(rows_here, C_IN)
            product = jnp.dot(shifted, stacked, preferred_element_type=jnp.float32)
            hidden = hidden.at[:, np.array(parity_ids), :].add(
                product.reshape(rows_here, len(parity_ids), C_OUT)
            )
        hidden = hidden + conv_bias
        upstream_cot = cot_block.astype(jnp.float32).reshape(
            block_size, FIELDS, PS, 2, PS, 2, PS, 2
        )
        upstream_cot = upstream_cot.transpose(0, 2, 4, 6, 3, 5, 7, 1).reshape(rows_here, 8, FIELDS)
        sigmoid_h = jax.nn.sigmoid(hidden)
        active = hidden * sigmoid_h
        upstream = jnp.einsum(
            "rqf,of->rqo", upstream_cot, head_weight, precision=lax.Precision.HIGHEST
        )
        grad_hidden = upstream * sigmoid_h * (1.0 + hidden * (1.0 - sigmoid_h))
        bias_sum = bias_sum + jnp.sum(grad_hidden, axis=(0, 1))
        head_sum = head_sum + jnp.einsum(
            "rqo,rqf->of", active, upstream_cot, precision=lax.Precision.HIGHEST
        )
        return ((bias_sum, head_sum), grad_hidden.astype(jnp.bfloat16))

    initial = (jnp.zeros((C_OUT,), jnp.float32), jnp.zeros((C_OUT, FIELDS), jnp.float32))
    totals, grad_blocks = lax.scan(block_terms, initial, (patch_blocks, cot_blocks))
    return (totals, grad_blocks.reshape(slot_count * PS**3, 8, C_OUT))


def channel_grads(work_patches, grad_fine, layout_plan, row_count):
    slot_count = work_patches.shape[0]
    channels = work_patches
    channels = channels.reshape(slot_count, PAD, PAD, PAD, row_count)
    result = jnp.zeros((row_count, TAPS, C_OUT), jnp.float32)
    for offsets, parity_ids, tap_ids in layout_plan:
        shifted = channels[
            :,
            offsets[0] : offsets[0] + PS,
            offsets[1] : offsets[1] + PS,
            offsets[2] : offsets[2] + PS,
            :,
        ].reshape(slot_count * PS**3, row_count)
        chosen = grad_fine[:, np.array(parity_ids), :].reshape(
            slot_count * PS**3, len(parity_ids) * C_OUT
        )
        product = lax.dot_general(
            shifted, chosen, (((0,), (0,)), ((), ())), preferred_element_type=jnp.float32
        )
        result = result.at[:, np.array(tap_ids), :].add(
            product.reshape(row_count, len(parity_ids), C_OUT)
        )
    return result


def on_device(patches, destination, cotangent, conv_weight, conv_bias, head_weight):
    owners = lax.axis_size("domain")
    my_index = lax.axis_index("domain")
    own_rows = patches.shape[0]
    train_rows = cotangent.shape[0]
    per_pair = (train_rows + owners - 1) // owners
    slot_total = owners * per_pair
    layout_plan = shift_plan()
    listing = lax.all_gather(destination, "domain", axis=0, tiled=True)
    trainer_ids = jnp.arange(owners, dtype=jnp.int32)
    pair_counts = jnp.sum(
        (listing.reshape(owners, own_rows)[:, :, None] == trainer_ids[None, None, :]).astype(
            jnp.int32
        ),
        axis=1,
    )
    own_hits = (destination[:, None] == trainer_ids[None, :]).astype(jnp.int32)
    local_rank = jnp.sum(jnp.cumsum(own_hits, axis=0) * own_hits, axis=1) - 1
    incoming = jnp.sum(pair_counts * (trainer_ids == my_index).astype(jnp.int32)[None, :], axis=1)
    starts_in = jnp.cumsum(incoming) - incoming
    slot_rank = jnp.arange(per_pair, dtype=jnp.int32)
    slot_live = (slot_rank[None, :] < incoming[:, None]).reshape(slot_total)
    slot_place = (starts_in[:, None] + slot_rank[None, :]).reshape(slot_total)
    zero_value = jnp.zeros((), jnp.bfloat16)
    clipped = jnp.minimum(slot_place, train_rows - 1)
    outgoing = jnp.where(slot_live[:, None, None], cotangent[clipped], zero_value)
    arrived = lax.all_to_all(
        outgoing.reshape(owners, per_pair, FIELDS, FINE),
        "domain",
        split_axis=0,
        concat_axis=0,
        tiled=True,
    )
    arrived = arrived.reshape(slot_total, FIELDS, FINE)
    work_cot = arrived[destination * per_pair + local_rank]
    totals, grad_fine = local_terms(
        patches, work_cot, conv_weight, conv_bias, head_weight, layout_plan
    )
    grad_scale = float((owners * own_rows * PS**3) ** (-0.5))
    shard_rows = conv_weight.shape[0] // owners
    grad_conv = lax.psum_scatter(
        channel_grads(patches, grad_fine, layout_plan, shard_rows * lax.axis_size("domain")),
        "domain",
        scatter_dimension=0,
        tiled=True,
    )
    bias_total, head_total = lax.psum((totals[0], totals[1]), "domain")
    return (grad_conv * grad_scale, bias_total * grad_scale, head_total * grad_scale)


def solution(mesh):
    placed = (
        P(("groups", "domain"), None, None),
        P(("groups", "domain")),
        P(("groups", "domain"), None, None),
        P(),
        P(),
        P(),
    )
    return jax.shard_map(
        on_device,
        mesh=mesh,
        in_specs=placed,
        out_specs=(P(("groups", "domain"), None, None), P("groups"), P("groups", None)),
        check_vma=False,
    )
```

profile of v0, /device:TPU:0, one launch (start us, length us, event | category | flops | bytes accessed | tf_op | source)
XLA Modules:
  0.0 236.1 jit_solution(15943022215353345464)
XLA Ops:
  10.0 13.8 %all-reduce = s32[256]{0:T(256)S(1)} all-reduce(s32[256]{0:T(256)S(1)} %dynamic-update-slice.11), channel_id=1, replica_groups=mesh['groups'=2,'domain'=16] {'domain'}, use_global_device_ids=true, to_apply=%add | all-reduce | flops 256 | bytes 2048
  26.7 3.5 %all-to-all-start = ((bf16[16,2,4,512]{3,2,1,0:T(4,128)(2,1)}), bf16[16,2,4,512]{3,2,1,0:T(4,128)(2,1)S(1)}, u32[]{:S(2)}, u32[]{:S(2)}) async-start(bf16[16,2,4,512]{3,2,1,0:T(4,128)(2,1)} %broadcast_select_fusion.1), calls=%async_computation | async-start | bytes 262144 | tf_op jit(solution)/shard_map/all_to_all | solution.py:138
  31.0 1.9 fusion.20
  42.9 4.1 %fusion.19 = (bf16[16,4,4,4,256]{4,0,3,2,1:T(8,128)(2,1)S(1)}, bf16[16,4,4,4,256]{4,0,3,2,1:T(8,128)(2,1)S(1)}, bf16[16,4,4,4,256]{4,0,3,2,1:T(8,128)(2,1)S(1)},...) fusion(bf16[16,5,5,5,256]{4,0,3,2,1:T(8,128)(2,1)} %bitcast.36), kind=kLoop, calls=%fused_computation.114 | loop fusion | bytes 8388608 | tf_op jit(solution)/shard_map/slice | solution.py:93
  52.3 2.1 copy.157
  54.4 2.0 reshape.552
  56.4 2.1 copy.158
  58.5 1.9 reshape.555
  61.5 2.0 reshape.558
  72.1 51.3 %while.25 = (s32[]{:T(128)}, f32[64]{0:T(128)S(1)}, f32[64,4]{0,1:T(4,128)}, bf16[2,512,8,64]{1,3,2,0:T(8,128)(2,1)}, bf16[2,8,4,512]{3,2,1,0:T(4,128)(2,1)}, /*...) while((s32[]{:T(128)}, f32[64]{0:T(128)S(1)}, ...), condition=%wide.region_15.16_spmd.clone.clone.clone.clone, body=%wide.region_6.15_spmd.sunk.clone.clone.clone.clone.sunk | while | flops 483230272 | bytes 43551044 | solution.py:83
  73.3 1.7 fusion.104
  89.3 3.7 %copy.173 = bf16[8,4,4,4,2,2,2,4]{3,2,1,0,7,6,5,4:T(4,128)(2,1)S(1)} copy(bf16[8,4,4,4,2,2,2,4]{0,6,3,5,2,4,1,7:T(2,128)(2,1)S(1)} %bitcast.309) | data formatting | bytes 65536 | tf_op jit(solution)/shard_map/while/body/eval_jaxpr/reshape | solution.py:69
  92.9 2.0 reshape.983
  99.0 1.7 fusion.104
  102.7 1.5 scatter_fusion
  114.9 3.7 %copy.173 = bf16[8,4,4,4,2,2,2,4]{3,2,1,0,7,6,5,4:T(4,128)(2,1)S(1)} copy(bf16[8,4,4,4,2,2,2,4]{0,6,3,5,2,4,1,7:T(2,128)(2,1)S(1)} %bitcast.309) | data formatting | bytes 65536 | tf_op jit(solution)/shard_map/while/body/eval_jaxpr/reshape | solution.py:69
  118.6 2.0 reshape.983
  126.2 1.5 gather_fusion.4
  131.9 2.4 %fusion.21 = f32[512,256]{1,0:T(8,128)} fusion(bf16[1024,512]{0,1:T(8,128)(2,1)S(1)} %bitcast.310, bf16[1024,256]{1,0:T(8,128)(2,1)} %reshape.552), kind=kOutput, calls=%fused_computation.116 | convolution fusion | flops 268435456 | bytes 2097152 | tf_op jit(solution)/shard_map/dot_general | solution.py:103
  141.4 1.7 scatter_fusion.8
  143.9 1.5 scatter_fusion.10
  148.8 4.4 %copy.148 = f32[256,27,64]{2,1,0:T(8,128)} copy(f32[256,27,64]{0,2,1:T(8,128)S(1)} %fusion.14) | data formatting | bytes 3538944 | tf_op jit(solution)/shard_map/scatter-add | solution.py:106
  153.9 33.9 %all-reduce.1 = (f32[64]{0:T(128)S(1)}, f32[64,4]{0,1:T(4,128)S(1)}) all-reduce(f32[64]{0:T(128)S(1)} %get-tuple-element.595, f32[64,4]{0,1:T(4,128)S(1)} %copy-done.49), channel_id=1, replica_groups=mesh['groups'=2,'domain'=16] {'domain'}, use_global_device_ids=true, to_apply=%region_25.26 | all-reduce | flops 320 | bytes 2560 | tf_op jit(solution)/shard_map/psum | solution.py:158
  188.9 38.6 %reduce-scatter.2.cloned.1.call-done = f32[16,27,64]{2,1,0:T(8,128)} async-done(((f32[256,27,64]{2,1,0:T(8,128)}), f32[16,27,64]{2,1,0:T(8,128)}) %reduce-scatter.2.cloned.1.call-update) | async-done | bytes 110608 | tf_op jit(solution)/shard_map/reduce_scatter | solution.py:152
  (293 shorter events, 86.6 us)
Async XLA Ops:
  7.2 18.1 %copy-start = (bf16[32,4,512]{2,1,0:T(4,128)(2,1)S(1)}, bf16[32,4,512]{2,1,0:T(4,128)(2,1)}, u32[]{:S(2)}) copy-start(bf16[32,4,512]{2,1,0:T(4,128)(2,1)} %param.62) | copy-start | bytes 393220
  7.2 27.1 %copy-start.46 = (s32[16]{0:T(128)S(1)}, s32[16]{0:T(128)}, u32[]{:S(2)}) copy-start(s32[16]{0:T(128)} %param.61) | copy-start | bytes 196
  26.7 44.2 %all-to-all-start = ((bf16[16,2,4,512]{3,2,1,0:T(4,128)(2,1)}), bf16[16,2,4,512]{3,2,1,0:T(4,128)(2,1)S(1)}, u32[]{:S(2)}, u32[]{:S(2)}) async-start(bf16[16,2,4,512]{3,2,1,0:T(4,128)(2,1)} %broadcast_select_fusion.1), calls=%async_computation | async-start | bytes 262144 | tf_op jit(solution)/shard_map/all_to_all | solution.py:138
  30.2 197.3 %reduce-scatter.2.cloned.1.call-start = ((), (), s32[]{:S(2)}) async-start(), calls=%async_computation.2 | async-start | bytes 4456448 | tf_op jit(solution)/shard_map/reduce_scatter | solution.py:152
  42.7 5.5 %copy-start.39 = (s32[2]{0:T(128)S(1)}, s32[2]{0:T(128)}, u32[]{:S(2)}) copy-start(s32[2]{0:T(128)} %constant.195.clone) | copy-start | bytes 28
  42.7 6.1 %copy-start.40 = (s32[2]{0:T(128)S(1)}, s32[2]{0:T(128)}, u32[]{:S(2)}) copy-start(s32[2]{0:T(128)} %constant.197.clone) | copy-start | bytes 28
  42.7 6.1 %copy-start.41 = (s32[2]{0:T(128)S(1)}, s32[2]{0:T(128)}, u32[]{:S(2)}) copy-start(s32[2]{0:T(128)} %constant.198.clone) | copy-start | bytes 28
  42.7 6.7 %copy-start.35 = (bf16[256,64]{0,1:T(8,128)(2,1)S(1)}, bf16[256,64]{0,1:T(8,128)(2,1)}, u32[]{:S(2)}) copy-start(bf16[256,64]{0,1:T(8,128)(2,1)} %get-tuple-element.993) | copy-start | bytes 98308
  42.8 6.7 %copy-start.36 = (bf16[256,64]{0,1:T(8,128)(2,1)S(1)}, bf16[256,64]{0,1:T(8,128)(2,1)}, u32[]{:S(2)}) copy-start(bf16[256,64]{0,1:T(8,128)(2,1)} %get-tuple-element.994) | copy-start | bytes 98308
  42.8 6.6 %copy-start.37 = (bf16[256,64]{0,1:T(8,128)(2,1)S(1)}, bf16[256,64]{0,1:T(8,128)(2,1)}, u32[]{:S(2)}) copy-start(bf16[256,64]{0,1:T(8,128)(2,1)} %get-tuple-element.999) | copy-start | bytes 98308
  42.8 6.6 %copy-start.38 = (bf16[256,64]{0,1:T(8,128)(2,1)S(1)}, bf16[256,64]{0,1:T(8,128)(2,1)}, u32[]{:S(2)}) copy-start(bf16[256,64]{0,1:T(8,128)(2,1)} %get-tuple-element.1000) | copy-start | bytes 98308
  42.8 7.3 %copy-start.31 = (bf16[256,64]{0,1:T(8,128)(2,1)S(1)}, bf16[256,64]{0,1:T(8,128)(2,1)}, u32[]{:S(2)}) copy-start(bf16[256,64]{0,1:T(8,128)(2,1)} %get-tuple-element.995) | copy-start | bytes 98308
  42.8 7.3 %copy-start.32 = (bf16[256,64]{0,1:T(8,128)(2,1)S(1)}, bf16[256,64]{0,1:T(8,128)(2,1)}, u32[]{:S(2)}) copy-start(bf16[256,64]{0,1:T(8,128)(2,1)} %get-tuple-element.996) | copy-start | bytes 98308
  42.8 7.3 %copy-start.33 = (bf16[256,64]{0,1:T(8,128)(2,1)S(1)}, bf16[256,64]{0,1:T(8,128)(2,1)}, u32[]{:S(2)}) copy-start(bf16[256,64]{0,1:T(8,128)(2,1)} %get-tuple-element.997) | copy-start | bytes 98308
  42.8 7.3 %copy-start.34 = (bf16[256,64]{0,1:T(8,128)(2,1)S(1)}, bf16[256,64]{0,1:T(8,128)(2,1)}, u32[]{:S(2)}) copy-start(bf16[256,64]{0,1:T(8,128)(2,1)} %get-tuple-element.998) | copy-start | bytes 98308
  42.8 8.0 %copy-start.24 = (bf16[256,64]{0,1:T(8,128)(2,1)S(1)}, bf16[256,64]{0,1:T(8,128)(2,1)}, u32[]{:S(2)}) copy-start(bf16[256,64]{0,1:T(8,128)(2,1)} %get-tuple-element.1004) | copy-start | bytes 98308
  42.8 8.0 %copy-start.25 = (bf16[256,64]{0,1:T(8,128)(2,1)S(1)}, bf16[256,64]{0,1:T(8,128)(2,1)}, u32[]{:S(2)}) copy-start(bf16[256,64]{0,1:T(8,128)(2,1)} %get-tuple-element.1005) | copy-start | bytes 98308
  42.8 8.0 %copy-start.26 = (bf16[256,64]{0,1:T(8,128)(2,1)S(1)}, bf16[256,64]{0,1:T(8,128)(2,1)}, u32[]{:S(2)}) copy-start(bf16[256,64]{0,1:T(8,128)(2,1)} %get-tuple-element.1006) | copy-start | bytes 98308
  42.9 7.9 %copy-start.27 = (bf16[256,64]{0,1:T(8,128)(2,1)S(1)}, bf16[256,64]{0,1:T(8,128)(2,1)}, u32[]{:S(2)}) copy-start(bf16[256,64]{0,1:T(8,128)(2,1)} %get-tuple-element.1007) | copy-start | bytes 98308
  42.9 7.9 %copy-start.28 = (bf16[256,64]{0,1:T(8,128)(2,1)S(1)}, bf16[256,64]{0,1:T(8,128)(2,1)}, u32[]{:S(2)}) copy-start(bf16[256,64]{0,1:T(8,128)(2,1)} %get-tuple-element.1008) | copy-start | bytes 98308
  88.9 6.0 %copy-start.57 = (f32[64,4]{0,1:T(4,128)S(1)}, f32[64,4]{0,1:T(4,128)}, u32[]{:S(2)}) copy-start(f32[64,4]{0,1:T(4,128)} %get-tuple-element.1196) | copy-start | bytes 3076 | tf_op jit(solution)/shard_map/while
  88.9 6.0 %copy-start.58 = (f32[64]{0:T(128)S(1)}, f32[64]{0:T(128)}, u32[]{:S(2)}) copy-start(f32[64]{0:T(128)} %get-tuple-element.1206) | copy-start | bytes 772 | tf_op jit(solution)/shard_map/while
  114.6 6.0 %copy-start.57 = (f32[64,4]{0,1:T(4,128)S(1)}, f32[64,4]{0,1:T(4,128)}, u32[]{:S(2)}) copy-start(f32[64,4]{0,1:T(4,128)} %get-tuple-element.1196) | copy-start | bytes 3076 | tf_op jit(solution)/shard_map/while
  114.6 6.0 %copy-start.58 = (f32[64]{0:T(128)S(1)}, f32[64]{0:T(128)}, u32[]{:S(2)}) copy-start(f32[64]{0:T(128)} %get-tuple-element.1206) | copy-start | bytes 772 | tf_op jit(solution)/shard_map/while
  (51 other events, 108.7 us)
Sparse Core Ops, SparseCore 0:
  153.4 74.0 reduce-scatter.1
where the time goes:
time: 238 us; the launch traced here: 236 us
  local copies, waits for them, and re-layouts  77.7 us (33%)
  blocking collectives  47.6 us (20%)
  waiting for transfers between devices  38.6 us (16%)
  other arithmetic  29.9 us (13%)
  matrix products  22.6 us (9%)
  between operations  15.3 us (6%)
  starting transfers between devices  3.55 us (1%)
    reduce_scatter x1, waiting for transfers between devices, on_device(): lax.psum_scatter(channel_grads(patches, grad_fine, layout_plan, shard_row...  38.6 us
    psum x1, blocking collectives, on_device(): bias_total, head_total = lax.psum((totals[0], totals[1]), 'domain')  33.9 us
    unnamed x110, local copies, waits for them, and re-layouts  20.8 us
    unnamed x1, blocking collectives  13.8 us
    scatter-add x14, other arithmetic, block_terms(): hidden.at[:, np.array(parity_ids), :]  13.5 us
    reshape x4, local copies, waits for them, and re-layouts, block_terms(): upstream_cot.transpose(0, 2, 4, 6, 3, 5, 7, 1).reshape(rows_here, 8, FIELDS)  11.3 us
    reshape x8, local copies, waits for them, and re-layouts, channel_grads(): shifted = channels[:, offsets[0]:offsets[0] + PS, offsets[1]:offsets[1] +...  10.5 us
    dot_general x16, matrix products, block_terms(): product = jnp.dot(shifted, stacked, preferred_element_type=jnp.float32)  9.47 us
  transfers between devices with their start and end apart: 2, of which 1 were waited for; matrix products, arithmetic and copies ran while one was open for 18% of the time, Pallas kernels for 0%

commit v1 on v0

v1 whole, which is shorter than its diff:
```python
import jax
import jax.numpy as jnp
import numpy as np
from jax import lax
from jax.experimental import pallas as pl
from jax.experimental.pallas import tpu as pltpu
from jax.sharding import PartitionSpec as P

C_IN = 256
C_OUT = 64
FIELDS = 4
TAPS = 27
PS = 4
PAD = 5
CELLS = PAD**3
FINE = 512
LANES = 128
BLOCKS = 14
SUM_ROWS = 16
F32 = jnp.float32
BF16 = jnp.bfloat16
HALF_TAPS = [(b * 3 + 1, b * 3 + 2) for b in range(9)]
HALF_TAPS += [(4 * 3, 7 * 3), (5 * 3, 8 * 3), (3 * 3, 6 * 3), (1 * 3, 2 * 3), (None, 0)]


def count_list(destination, owners):
    own = destination.shape[0]

    def body(dest_ref, out_ref):
        trainer = lax.broadcasted_iota(jnp.int32, (owners, LANES), 0)
        total = jnp.zeros((owners, LANES), jnp.int32)
        for n in range(own):
            total = total + (trainer == dest_ref[n]).astype(jnp.int32)
        out_ref[...] = total.reshape(owners, 1, LANES)

    return pl.pallas_call(
        body,
        in_specs=[pl.BlockSpec(memory_space=pltpu.SMEM)],
        out_specs=pl.BlockSpec(memory_space=pltpu.VMEM),
        out_shape=jax.ShapeDtypeStruct((owners, 1, LANES), jnp.int32),
        name="count_list",
    )(destination)


def row_copy(counts, rows, per_pair):
    owners = counts.shape[0]
    limit = rows.shape[0] - 1

    def body(count_ref, rows_ref, out_ref):
        def one_owner(owner, start):
            for rank in range(per_pair):
                out_ref[owner * per_pair + rank] = rows_ref[jnp.minimum(start + rank, limit)]
            return start + count_ref[owner, 0, 0]

        lax.fori_loop(0, owners, one_owner, jnp.int32(0))

    return pl.pallas_call(
        body,
        in_specs=[
            pl.BlockSpec(memory_space=pltpu.SMEM),
            pl.BlockSpec(memory_space=pltpu.VMEM),
        ],
        out_specs=pl.BlockSpec(memory_space=pltpu.VMEM),
        out_shape=jax.ShapeDtypeStruct((owners * per_pair,) + rows.shape[1:], rows.dtype),
        name="row_copy",
    )(counts, rows)


def head_terms(head):
    rows = jnp.concatenate([jnp.broadcast_to(head[f : f + 1], (32, C_OUT)) for f in range(FIELDS)], axis=0)
    pair = jnp.concatenate([rows, rows], axis=1)
    table = jnp.concatenate([pair] * 4, axis=1)
    row = lax.broadcasted_iota(jnp.int32, table.shape, 0)
    col = lax.broadcasted_iota(jnp.int32, table.shape, 1)
    table = jnp.where(row % 8 == col // C_OUT, table, 0.0)
    high = table.astype(BF16)
    return high, (table - high.astype(F32)).astype(BF16)


def forward_part(patches, first, count, weights, bias, destination, head, per_pair):
    own = patches.shape[1]
    rows = 16 * own
    lead = first == 0

    def body(*refs):
        dest_ref, head_ref, x_ref, w_ref, bias_ref = refs[:5]
        xt_ref, dact_ref, act_ref = refs[5:8]
        w2_ref = refs[-1]
        step = pl.program_id(0)

        @pl.when(step == 0)
        def _():
            w2_ref[1, :, 0:C_OUT, :] = jnp.zeros((9, C_OUT, C_IN), BF16)
            for b in range(9):
                w2_ref[0, b] = w_ref[3 * b + 1 : 3 * b + 3].reshape(2 * C_OUT, C_IN)
                w2_ref[1, b, C_OUT:, :] = w_ref[3 * b]
            if lead:
                places_ref, table_ref = refs[8:10]
                for n in range(own):
                    rank = jnp.int32(0)
                    for k in range(n):
                        rank = rank + (dest_ref[k] == dest_ref[n]).astype(jnp.int32)
                    places_ref[n] = dest_ref[n] * per_pair + rank
                table_ref[0], table_ref[1] = head_terms(head_ref[...])

        m1 = step + first
        picked = []
        for shift in range(8):
            s1, s2, s3 = shift // 4, (shift // 2) % 2, shift % 2
            pieces = [
                x_ref[pl.ds((m1 + s1) * 25 + (m2 + s2) * 5 + s3, 4)].reshape(4 * own, C_IN)
                for m2 in range(4)
            ]
            value = jnp.concatenate(pieces, axis=0)
            picked.append(value)
            xt_ref[shift] = value.T
        bias_row = jnp.concatenate([bias_ref[...]] * 4, axis=1)
        for p1 in range(2):
            both = jnp.zeros((rows, 2 * LANES), F32)
            odd = jnp.zeros((rows, LANES), F32)
            for s1 in range(p1 + 1):
                k1 = 1 if p1 == 0 else (2 if s1 == 0 else 0)
                for s3 in range(2):
                    both = both + lax.dot_general(
                        picked[s1 * 4 + s3],
                        w2_ref[s3, k1 * 3 + 1 : k1 * 3 + 3].reshape(2 * LANES, C_IN),
                        (((1,), (1,)), ((), ())),
                        preferred_element_type=F32,
                    )
                    odd = odd + lax.dot_general(
                        picked[s1 * 4 + 2 + s3],
                        w2_ref[s3, k1 * 3],
                        (((1,), (1,)), ((), ())),
                        preferred_element_type=F32,
                    )
            hidden = jnp.concatenate([both[:, :LANES], both[:, LANES:] + odd], axis=1) + bias_row
            gate = jax.nn.sigmoid(hidden)
            active = hidden * gate
            lanes = slice(p1 * 2 * LANES, (p1 + 1) * 2 * LANES)
            dact_ref[:, lanes] = gate * (1.0 + hidden * (1.0 - gate))
            high = active.astype(BF16)
            act_ref[0, :, lanes] = high
            act_ref[1, :, lanes] = (active - high.astype(F32)).astype(BF16)

    fixed = lambda *shape: pl.BlockSpec(shape, lambda i: (0,) * len(shape))
    out_specs = [
        pl.BlockSpec((8, C_IN, rows), lambda i: (0, 0, i)),
        pl.BlockSpec((rows, 512), lambda i: (i, 0)),
        pl.BlockSpec((2, rows, 512), lambda i: (0, i, 0)),
    ]
    out_shape = [
        jax.ShapeDtypeStruct((8, C_IN, count * rows), BF16),
        jax.ShapeDtypeStruct((count * rows, 512), F32),
        jax.ShapeDtypeStruct((2, count * rows, 512), BF16),
    ]
    if lead:
        out_specs += [pl.BlockSpec(memory_space=pltpu.SMEM), fixed(2, LANES, 512)]
        out_shape += [
            jax.ShapeDtypeStruct((own,), jnp.int32),
            jax.ShapeDtypeStruct((2, LANES, 512), BF16),
        ]
    return pl.pallas_call(
        body,
        grid=(count,),
        in_specs=[
            pl.BlockSpec(memory_space=pltpu.SMEM),
            fixed(FIELDS, C_OUT),
            fixed(CELLS, own, C_IN),
            fixed(TAPS, C_OUT, C_IN),
            fixed(1, C_OUT),
        ],
        out_specs=out_specs,
        out_shape=out_shape,
        scratch_shapes=[pltpu.VMEM((2, 9, LANES, C_IN), BF16)],
        cost_estimate=pl.CostEstimate(
            flops=count * 2 * rows * C_IN * 3600, transcendentals=0, bytes_accessed=4 << 20
        ),
        name="forward_part",
    )(destination, head, patches, weights, bias)


def split_sums(sums):
    high = sums.astype(BF16)
    rest = sums - high.astype(F32)
    middle = rest.astype(BF16)
    low = (rest - middle.astype(F32)).astype(BF16)
    low_lanes = lax.broadcasted_iota(jnp.int32, sums.shape, 1) < C_OUT
    first = jnp.where(low_lanes, high.astype(F32), pltpu.roll(middle.astype(F32), C_OUT, 1))
    second = jnp.where(low_lanes, low.astype(F32), 0.0)
    return jnp.concatenate([first, second], axis=0).astype(BF16)


def join_sums(rows):
    return rows[0:8] + pltpu.roll(rows[0:8], C_OUT, 1) + rows[8:16]


def backward(places, core, arrived, head_table, parts, slots):
    part_count = len(parts)
    part_rows = parts[0][1].shape[0]
    rows = part_count * part_rows
    steps = part_rows // (16 * slots)
    span = 16 * slots
    groups = C_IN // 32

    def body(*refs):
        places_ref, core_ref, arrived_ref, head_ref = refs[:4]
        sources = refs[4 : 4 + 3 * part_count]
        keep_ref, send_ref, sums_ref = refs[4 + 3 * part_count : 7 + 3 * part_count]
        xt_ref, dact_ref, act_ref, dsel_ref, grad_ref, pack_ref, sem = refs[7 + 3 * part_count :]
        copies = []
        for part in range(part_count):
            xt_hbm, dact_hbm, act_hbm = sources[3 * part : 3 * part + 3]
            copies.append(
                (
                    pltpu.make_async_copy(dact_hbm, dact_ref.at[part], sem.at[0, part]),
                    pltpu.make_async_copy(act_hbm, act_ref.at[part], sem.at[1, part]),
                    pltpu.make_async_copy(xt_hbm, xt_ref.at[part], sem.at[2, part]),
                )
            )
        for kind in range(3):
            for part in range(part_count):
                copies[part][kind].start()
        for n in range(slots):
            dsel_ref[:, n, :] = arrived_ref[places_ref[n]].astype(F32)
        fields = dsel_ref[...].reshape(span, LANES).astype(BF16)
        lane = lax.broadcasted_iota(jnp.int32, (1, LANES), 1)
        low_lanes = lane < C_OUT
        bias_sum = jnp.zeros((1, 512), F32)
        head_sum = jnp.zeros((LANES, 512), F32)
        for part in range(part_count):
            copies[part][0].wait()
            copies[part][1].wait()
            for step in range(steps):
                m1 = part * steps + step
                here = slice(step * span, (step + 1) * span)
                there = slice(m1 * span, (m1 + 1) * span)
                mine = (lane // 8) % 4 == m1
                some = jnp.where(mine, fields, jnp.zeros_like(fields))
                upstream = jnp.dot(some, head_ref[0], preferred_element_type=F32)
                upstream = upstream + jnp.dot(some, head_ref[1], preferred_element_type=F32)
                grad = upstream * dact_ref[part, here, :]
                bias_sum = bias_sum + jnp.sum(grad, axis=0, keepdims=True)
                grad_ref[there, :] = grad.astype(BF16)
                blk = [grad[:, b * LANES : (b + 1) * LANES] for b in range(4)]
                for k, (lo, hi) in enumerate(((0, 2), (1, 3), (2, 3))):
                    packed = jnp.where(low_lanes, pltpu.roll(blk[lo], C_OUT, 1), blk[hi])
                    pack_ref[there, k * LANES : (k + 1) * LANES] = packed.astype(BF16)
                for term in range(2):
                    head_sum = head_sum + lax.dot_general(
                        some,
                        act_ref[part, term, here, :],
                        (((0,), (0,)), ((), ())),
                        preferred_element_type=F32,
                    )
        row = lax.broadcasted_iota(jnp.int32, (LANES, 512), 0)
        col = lax.broadcasted_iota(jnp.int32, (LANES, 512), 1)
        head_sum = jnp.where(row % 8 == col // C_OUT, head_sum, 0.0)
        heads = [
            jnp.sum(head_sum[f * 32 : (f + 1) * 32], axis=0, keepdims=True) for f in range(FIELDS)
        ]
        stacked = jnp.concatenate([bias_sum] + heads + [jnp.zeros((3, 512), F32)], axis=0)
        folded = sum(stacked[:, b * LANES : (b + 1) * LANES] for b in range(4))
        folded = folded + pltpu.roll(folded, C_OUT, 1)
        sums_ref[...] = folded
        send_ref[groups * BLOCKS * 16 :, :] = split_sums(folded)
        mine_core = core_ref[0]
        for part in range(part_count):
            copies[part][2].wait()

        def product(shift, at_ref, lanes):
            result = None
            for part in range(part_count):
                term = jnp.dot(
                    xt_ref[part, shift],
                    at_ref[part * part_rows : (part + 1) * part_rows, lanes],
                    preferred_element_type=F32,
                )
                result = term if result is None else result + term
            return result

        def put(block, value):
            split = value.reshape(groups, 2, 16, LANES)
            even, odd = split[:, 0], split[:, 1]
            keep_ref[:, block * 16 : (block + 1) * 16, :] = jnp.where(mine_core == 0, even, odd)
            other = jnp.where(mine_core == 0, odd, even).astype(BF16)
            for g in range(groups):
                send_ref[(g * BLOCKS + block) * 16 : (g * BLOCKS + block + 1) * 16, :] = other[g]

        for shift, lo, count, blocks in (
            (0, 0, 2, (4, 5)),
            (0, 2, 2, (7, 8)),
            (4, 2, 2, (1, 2)),
            (6, 3, 1, (0,)),
        ):
            value = product(shift, grad_ref, slice(lo * LANES, (lo + count) * LANES))
            for k, block in enumerate(blocks):
                put(block, value[:, k * LANES : (k + 1) * LANES])
        put(3, product(2, grad_ref, slice(LANES, 2 * LANES)))
        put(6, product(2, grad_ref, slice(3 * LANES, 4 * LANES)))
        value = product(1, pack_ref, slice(0, 2 * LANES))
        put(9, value[:, 0:LANES])
        put(10, value[:, LANES:])
        put(11, product(3, pack_ref, slice(LANES, 2 * LANES)))
        put(12, product(5, pack_ref, slice(2 * LANES, 3 * LANES)))
        put(13, product(7, pack_ref, slice(LANES, 2 * LANES)))

    smem = pl.BlockSpec(memory_space=pltpu.SMEM)
    vmem = pl.BlockSpec(memory_space=pltpu.VMEM)
    hbm = pl.BlockSpec(memory_space=pl.ANY)
    return pl.pallas_call(
        body,
        in_specs=[smem, smem, vmem, vmem] + [hbm] * (3 * part_count),
        out_specs=[vmem, vmem, vmem],
        out_shape=[
            jax.ShapeDtypeStruct((groups, BLOCKS * 16, LANES), F32),
            jax.ShapeDtypeStruct((groups * BLOCKS * 16 + SUM_ROWS, LANES), BF16),
            jax.ShapeDtypeStruct((8, LANES), F32),
        ],
        scratch_shapes=[
            pltpu.VMEM((part_count, 8, C_IN, part_rows), BF16),
            pltpu.VMEM((part_count, part_rows, 512), F32),
            pltpu.VMEM((part_count, 2, part_rows, 512), BF16),
            pltpu.VMEM((16, slots, LANES), F32),
            pltpu.VMEM((rows, 512), BF16),
            pltpu.VMEM((rows, 3 * LANES), BF16),
            pltpu.SemaphoreType.DMA((3, part_count)),
        ],
        name="backward",
    )(places, core, arrived, head_table, *[a for part in parts for a in part])


def pair_sum(keep, sums, other):
    groups, block_rows, _ = keep.shape

    def body(keep_ref, sums_ref, other_ref, out_ref):
        theirs = join_sums(other_ref[groups * block_rows :, :].astype(F32))
        tail = split_sums(sums_ref[...] + theirs)
        for g in range(groups):
            partner = other_ref[g * block_rows : (g + 1) * block_rows, :].astype(F32)
            out_ref[g, 0:block_rows, :] = (keep_ref[g] + partner).astype(BF16)
            out_ref[g, block_rows:, :] = tail

    return pl.pallas_call(
        body,
        out_shape=jax.ShapeDtypeStruct((groups, block_rows + SUM_ROWS, LANES), BF16),
        name="pair_sum",
    )(keep, sums, other)


def final_sum(arrived, scale, per_block):
    sources, all_rows, _ = arrived.shape
    block_rows = all_rows - SUM_ROWS

    def body(in_ref, conv_ref, bias_ref, head_ref):
        total = in_ref[0].astype(F32)
        for source in range(1, sources):
            total = total + in_ref[source].astype(F32)
        total = total * scale
        for block, taps in enumerate(HALF_TAPS):
            for half, tap in enumerate(taps):
                if tap is not None:
                    conv_ref[tap] = total[
                        block * per_block : (block + 1) * per_block, half * C_OUT : (half + 1) * C_OUT
                    ]
        joined = join_sums(total[block_rows:])
        bias_ref[...] = joined[0:1, 0:C_OUT]
        head_ref[...] = joined[1 : 1 + FIELDS, 0:C_OUT]

    return pl.pallas_call(
        body,
        out_shape=[
            jax.ShapeDtypeStruct((TAPS, per_block, C_OUT), F32),
            jax.ShapeDtypeStruct((1, C_OUT), F32),
            jax.ShapeDtypeStruct((FIELDS, C_OUT), F32),
        ],
        name="final_sum",
    )(arrived)


def on_device(patches, destination, cotangent, conv_weight, conv_bias, head_weight):
    owners = lax.axis_size("domain")
    my_index = lax.axis_index("domain")
    own_rows = patches.shape[0]
    train_rows = cotangent.shape[0]
    per_pair = (train_rows + owners - 1) // owners
    channels = C_IN // owners
    splits = 16 // channels
    if splits > 1:
        order = np.arange(C_IN).reshape(C_IN // 32, splits, 2, channels)
        order = order.transpose(0, 2, 1, 3).reshape(-1)
        patches = patches[:, :, order]
        conv_weight = conv_weight[order]

    counts = lax.all_to_all(
        count_list(destination, owners), "domain", split_axis=0, concat_axis=0, tiled=True
    )

    rows = cotangent.reshape(train_rows, FIELDS, 4, 2, 4, 2, 4, 2)
    rows = rows.transpose(0, 4, 6, 1, 2, 3, 5, 7).reshape(train_rows, 16, LANES)
    outgoing = row_copy(counts, rows, per_pair)
    arrived = lax.all_to_all(
        outgoing.reshape(owners, per_pair, 16, LANES), "domain", split_axis=0, concat_axis=0, tiled=True
    ).reshape(owners * per_pair, 16, LANES)

    cells = patches.transpose(1, 0, 2)
    weights = conv_weight.transpose(1, 2, 0)
    parts = [
        forward_part(
            cells, first, 2, weights, conv_bias.reshape(1, C_OUT), destination, head_weight.T, per_pair
        )
        for first in (0, 2)
    ]
    places, head_table = parts[0][3:]
    parts = [part[:3] for part in parts]
    core = (my_index % 2).astype(jnp.int32).reshape(1)
    keep, send, sums = backward(places, core, arrived, head_table, parts, own_rows)
    other = lax.ppermute(send, "domain", [(i, i ^ 1) for i in range(owners)])
    payload = pair_sum(keep, sums, other)

    scale = float((owners * own_rows * PS**3) ** (-0.5))
    mates = owners // 2
    groups = [[core_id + 2 * k for k in range(mates)] for core_id in range(2)]
    block_rows = BLOCKS * 16
    if splits > 1:
        tail = jnp.repeat(payload[:, block_rows:], splits, axis=0)
        blocks = payload[:, :block_rows].reshape(C_IN // 32, BLOCKS, splits, channels, LANES)
        blocks = blocks.transpose(0, 2, 1, 3, 4).reshape(mates, BLOCKS * channels, LANES)
        payload = jnp.concatenate([blocks, tail], axis=1)
    swapped = lax.all_to_all(
        payload, "domain", split_axis=0, concat_axis=0, tiled=True, axis_index_groups=groups
    )
    if splits > 1:
        tail = jnp.sum(swapped[:, BLOCKS * channels :].astype(F32), axis=0) * scale
        tail = tail[0:8, 0:C_OUT] + tail[0:8, C_OUT:] + tail[8:, 0:C_OUT]
        total = jnp.sum(swapped[:, : BLOCKS * channels].astype(F32), axis=0) * scale
        total = total.reshape(BLOCKS, channels, 2, C_OUT)
        where = {tap: (b, h) for b, pair in enumerate(HALF_TAPS) for h, tap in enumerate(pair)}
        conv = jnp.stack([total[where[t][0], :, where[t][1]] for t in range(TAPS)], axis=1)
        return conv, tail[0], tail[1 : 1 + FIELDS].T
    conv, bias_out, head_out = final_sum(swapped, scale, channels)
    return conv.transpose(1, 0, 2), bias_out.reshape(C_OUT), head_out.T


def solution(mesh):
    placed = (
        P(("groups", "domain"), None, None),
        P(("groups", "domain")),
        P(("groups", "domain"), None, None),
        P(),
        P(),
        P(),
    )
    return jax.shard_map(
        on_device,
        mesh=mesh,
        in_specs=placed,
        out_specs=(P(("groups", "domain"), None, None), P("groups"), P("groups", None)),
        check_vma=False,
    )
```

time: 238 us -> 66.2 us (0.28)
  local copies, waits for them, and re-layouts: 77.7 us -> 4.56 us
  waiting for transfers between devices: 38.6 us -> 5.65 us
  other arithmetic: 29.9 us -> 0 us
  blocking collectives: 47.6 us -> 20 us
  Pallas kernels: 0 us -> 23.4 us
  matrix products: 22.6 us -> 0 us
  between operations: 15.3 us -> 0.71 us
  starting transfers between devices: 3.55 us -> 11.2 us
    reduce_scatter x1 -> x0, waiting for transfers between devices: 38.6 us -> none  [on_device(): lax.psum_scatter(channel_grads(patches, grad_fine, layout_plan, shard_row...]
    psum x1 -> x0, blocking collectives: 33.9 us -> none  [on_device(): bias_total, head_total = lax.psum((totals[0], totals[1]), 'domain')]
    reshape x29 -> x1, local copies, waits for them, and re-layouts: 26.1 us -> 0.88 us  [on_device(): rows = rows.transpose(0, 4, 6, 1, 2, 3, 5, 7).reshape(train_rows, 16, LANES)]
    pallas_call x0 -> x7, Pallas kernels: none -> 23.4 us  [the longest x2 9.11 us: forward_part(): pl.pallas_call(body, grid=(count,), in_specs=[pl.BlockSpec(memory_space=p...]
    dot_general x28 -> x0, matrix products: 22.6 us -> none  [the longest x16 9.47 us: block_terms(): product = jnp.dot(shifted, stacked, preferred_element_type=jnp.float32)]
    scatter-add x21 -> x0, other arithmetic: 20.5 us -> none  [the longest x14 13.5 us: block_terms(): hidden.at[:, np.array(parity_ids), :]]
    all_to_all x0 -> x1, blocking collectives: none -> 20 us  [on_device(): lax.all_to_all(payload, 'domain', split_axis=0, concat_axis=0, tiled=True...]
    unnamed x110 -> x7, local copies, waits for them, and re-layouts: 20.8 us -> 3.21 us
  transfers between devices with their start and end apart: 2 -> 3, of which waited for: 1 -> 2; matrix products, arithmetic and copies ran while one was open for 18% -> 4% of each run, Pallas kernels for 0% -> 14%
where the time goes in v1:
time: 66.2 us; the launch traced here: 65.6 us
  Pallas kernels  23.4 us (35%)
  blocking collectives  20 us (30%)
  starting transfers between devices  11.2 us (17%)
  waiting for transfers between devices  5.65 us (9%)
  local copies, waits for them, and re-layouts  4.56 us (7%)
  between operations  0.71 us (1%)
    all_to_all x1, blocking collectives, on_device(): lax.all_to_all(payload, 'domain', split_axis=0, concat_axis=0, tiled=True...  20 us
    pallas_call x2, Pallas kernels, forward_part(): pl.pallas_call(body, grid=(count,), in_specs=[pl.BlockSpec(memory_space=p...  9.11 us
    all_to_all x1, starting transfers between devices, on_device(): lax.all_to_all(count_list(destination, owners), 'domain', split_axis=0, c...  7.41 us
    pallas_call x1, Pallas kernels, backward(): pl.pallas_call(body, in_specs=[smem, smem, vmem, vmem] + [hbm] * (3 * par...  7.25 us
    all_to_all x1, waiting for transfers between devices, on_device(): lax.all_to_all(count_list(destination, owners), 'domain', split_axis=0, c...  3.88 us
    all_to_all x1, starting transfers between devices, on_device(): lax.all_to_all(outgoing.reshape(owners, per_pair, 16, LANES), 'domain', s...  3.51 us
    unnamed x7, local copies, waits for them, and re-layouts  3.21 us
    pallas_call x1, Pallas kernels, pair_sum(): pl.pallas_call(body, out_shape=jax.ShapeDtypeStruct((groups, block_rows +...  2.24 us
  transfers between devices with their start and end apart: 3, of which 2 were waited for; matrix products, arithmetic and copies ran while one was open for 4% of the time, Pallas kernels for 14%

profile of v1, /device:TPU:0, one launch (start us, length us, event | category | flops | bytes accessed | tf_op | source)
XLA Modules:
  0.0 65.6 jit_solution(10353402858295144416)
XLA Ops:
  0.6 1.3 %count_list.1 = s32[16,1,128]{2,1,0:T(1,128)} custom-call(s32[16]{0:T(128)} %refs_0_.3), custom_call_target="tpu_custom_call" | custom-call | tf_op jit(solution)/shard_map/count_list/pallas_call | solution.py:36
  1.9 7.4 %all-to-all-start = ((s32[16,1,128]{2,1,0:T(1,128)}), s32[16,1,128]{2,1,0:T(1,128)S(1)}, u32[]{:S(2)}, u32[]{:S(2)}) async-start(s32[16,1,128]{2,1,0:T(1,128)} %count_list.1), calls=%async_computation | async-start | bytes 16384 | tf_op jit(solution)/shard_map/all_to_all | solution.py:394
  9.3 1.2 %copy.10 = bf16[32,4,512]{0,2,1:T(8,128)(2,1)S(1)} copy(bf16[32,4,512]{2,1,0:T(4,128)(2,1)} %param.8) | data formatting | bytes 262144 | tf_op args[2]
  10.5 0.5 copy.11
  11.0 0.9 %copy.12.rows_ref = bf16[32,16,128]{2,1,0:T(8,128)(2,1)} copy(bf16[32,16,128]{0,2,1:T(8,128)(2,1)S(1)} %bitcast.14) | data formatting | bytes 262144 | tf_op jit(solution)/shard_map/reshape | solution.py:399
  11.9 3.9 %all-to-all-done.count_ref = s32[16,1,128]{2,1,0:T(1,128)S(1)} async-done(((s32[16,1,128]{2,1,0:T(1,128)}), s32[16,1,128]{2,1,0:T(1,128)S(1)}, u32[]{:S(2)}, u32[]{:S(2)}) %all-to-all-start) | async-done | bytes 8224 | tf_op jit(solution)/shard_map/all_to_all | solution.py:394
  15.8 0.0 copy-start.2
  15.8 0.6 copy-done.2
  16.4 1.7 %row_copy.1 = bf16[32,16,128]{2,1,0:T(8,128)(2,1)} custom-call(s32[16,1,128]{2,1,0:T(1,128)} %copy-done.2, bf16[32,16,128]{2,1,0:T(8,128)(2,1)} %copy.12.rows_ref), custom_call_target="tpu_custom_call" | custom-call | tf_op jit(solution)/shard_map/row_copy/pallas_call | solution.py:57
  18.1 3.5 %all-to-all-start.1 = ((bf16[16,2,16,128]{3,2,1,0:T(8,128)(2,1)}), bf16[16,2,16,128]{3,2,1,0:T(8,128)(2,1)S(1)}, u32[]{:S(2)}, u32[]{:S(2)}) async-start(bf16[16,2,16,128]{3,2,1,0:T(8,128)(2,1)} %bitcast.17), calls=%async_computation.1 | async-start | bytes 262144 | tf_op jit(solution)/shard_map/all_to_all | solution.py:401
  21.6 4.4 %forward_part.3 = (bf16[8,256,512]{2,1,0:T(8,128)(2,1)}, f32[512,512]{1,0:T(8,128)}, bf16[2,512,512]{2,1,0:T(8,128)(2,1)}) custom-call(s32[16]{0:T(128)} %refs_0_.3, f32[4,64]{1,0:T(4,128)} %bitcast.23, bf16[125,16,256]{2,1,0:T(8,128)(2,1)} %bitcast.18, bf16[27,64,256]{2,1,0:T(8,128)(2,1)} %bitcast.20, f32[1,64]{1,0:T(1,128)} %bitcast.26), custom_call_target="tpu_custom_call" | custom-call | flops 943718400 | bytes 4194304 | tf_op jit(solution)/shard_map/forward_part/pallas_call | solution.py:162
  26.0 4.7 %forward_part.2 = (bf16[8,256,512]{2,1,0:T(8,128)(2,1)}, f32[512,512]{1,0:T(8,128)}, bf16[2,512,512]{2,1,0:T(8,128)(2,1)}, s32[16]{0:T(128)}, bf16[2,128,512]{2,1,0:T(8,128)(2,1)}) custom-call(s32[16]{0:T(128)} %refs_0_.3, f32[4,64]{1,0:T(4,128)} %bitcast.24, bf16[125,16,256]{2,1,0:T(8,128)(2,1)} %bitcast.19, bf16[27,64,256]{2,1,0:T(8,128)(2,1)} %bitcast.21, ...), custom_call_target="tpu_custom_call" | custom-call | flops 943718400 | bytes 4194304 | tf_op jit(solution)/shard_map/forward_part/pallas_call | solution.py:162
  30.7 0.0 all-to-all-done.1
  30.7 0.0 copy-start
  30.7 0.6 copy-done
  31.4 7.2 %backward.1 = (f32[8,224,128]{2,1,0:T(8,128)}, bf16[1808,128]{1,0:T(8,128)(2,1)}, f32[8,128]{1,0:T(8,128)}) custom-call(s32[16]{0:T(128)} %get-tuple-element.17.refs_0_, s32[1]{0:T(128)} %bitcast.4.refs_1_, bf16[32,16,128]{2,1,0:T(8,128)(2,1)} %bitcast.16, bf16[2,128,512]{2,1,0:T(8,128)(2,1)} %get-tuple-element.18.refs_3_, ...), custom_call_target="tpu_custom_call" | custom-call | tf_op jit(solution)/shard_map/backward/pallas_call | solution.py:310
  38.6 0.3 collective-permute-start
  39.0 1.8 %collective-permute-done.other_ref = bf16[1808,128]{1,0:T(8,128)(2,1)S(1)} collective-permute-done((bf16[1808,128]{1,0:T(8,128)(2,1)}, bf16[1808,128]{1,0:T(8,128)(2,1)S(1)}, u32[]{:S(2)}, u32[]{:S(2)}) %collective-permute-start) | collective-permute-done | bytes 462880 | tf_op jit(solution)/shard_map/ppermute | solution.py:417
  40.7 0.0 copy-start.1
  40.7 0.8 %copy-done.1 = bf16[1808,128]{1,0:T(8,128)(2,1)} copy-done((bf16[1808,128]{1,0:T(8,128)(2,1)}, bf16[1808,128]{1,0:T(8,128)(2,1)S(1)}, u32[]{:S(2)}) %copy-start.1) | copy-done | bytes 462872
  41.5 2.2 %pair_sum.1 = bf16[8,240,128]{2,1,0:T(8,128)(2,1)} custom-call(f32[8,224,128]{2,1,0:T(8,128)} %get-tuple-element.25.keep_ref, f32[8,128]{1,0:T(8,128)} %get-tuple-element.26.sums_ref, bf16[1808,128]{1,0:T(8,128)(2,1)} %copy-done.1), custom_call_target="tpu_custom_call" | custom-call | tf_op jit(solution)/shard_map/pair_sum/pallas_call | solution.py:343
  43.8 20.0 %all_to_all.15.in_ref = bf16[8,240,128]{2,1,0:T(8,128)(2,1)} all-to-all(bf16[8,240,128]{2,1,0:T(8,128)(2,1)} %pair_sum.1), channel_id=1, replica_groups={{0,2,4,6,8,10,12,14},{1,3,5,7,9,11,13,15},{16,18,20,22,24,26,28,30},{17..., dimensions={0} | all-to-all | bytes 983040 | tf_op jit(solution)/shard_map/all_to_all | solution.py:429
  63.8 1.9 %final_sum.1 = (f32[27,16,64]{2,1,0:T(8,128)}, f32[1,64]{1,0:T(1,128)}, f32[4,64]{1,0:T(4,128)}) custom-call(bf16[8,240,128]{2,1,0:T(8,128)(2,1)} %all_to_all.15.in_ref), custom_call_target="tpu_custom_call" | custom-call | tf_op jit(solution)/shard_map/final_sum/pallas_call | solution.py:369
Async XLA Ops:
  1.9 13.9 %all-to-all-start = ((s32[16,1,128]{2,1,0:T(1,128)}), s32[16,1,128]{2,1,0:T(1,128)S(1)}, u32[]{:S(2)}, u32[]{:S(2)}) async-start(s32[16,1,128]{2,1,0:T(1,128)} %count_list.1), calls=%async_computation | async-start | bytes 16384 | tf_op jit(solution)/shard_map/all_to_all | solution.py:394
  15.8 0.6 copy-start.2
  18.1 12.6 %all-to-all-start.1 = ((bf16[16,2,16,128]{3,2,1,0:T(8,128)(2,1)}), bf16[16,2,16,128]{3,2,1,0:T(8,128)(2,1)S(1)}, u32[]{:S(2)}, u32[]{:S(2)}) async-start(bf16[16,2,16,128]{3,2,1,0:T(8,128)(2,1)} %bitcast.17), calls=%async_computation.1 | async-start | bytes 262144 | tf_op jit(solution)/shard_map/all_to_all | solution.py:401
  30.7 0.7 %copy-start = (bf16[16,2,16,128]{3,2,1,0:T(8,128)(2,1)}, bf16[16,2,16,128]{3,2,1,0:T(8,128)(2,1)S(1)}, u32[]{:S(2)}) copy-start(bf16[16,2,16,128]{3,2,1,0:T(8,128)(2,1)S(1)} %all-to-all-done.1) | copy-start | bytes 393220
  38.6 2.1 %collective-permute-start = (bf16[1808,128]{1,0:T(8,128)(2,1)}, bf16[1808,128]{1,0:T(8,128)(2,1)S(1)}, u32[]{:S(2)}, u32[]{:S(2)}) collective-permute-start(bf16[1808,128]{1,0:T(8,128)(2,1)} %get-tuple-element.27), channel_id=1, source_target_pairs={{0,1},{1,0},{2,3},{3,2},{4,5},{5,4},{6,7},{7,6},{8,9},{9,8},{10,11... | collective-permute-start | bytes 1388552 | tf_op jit(solution)/shard_map/ppermute | solution.py:417
  40.7 0.8 %copy-start.1 = (bf16[1808,128]{1,0:T(8,128)(2,1)}, bf16[1808,128]{1,0:T(8,128)(2,1)S(1)}, u32[]{:S(2)}) copy-start(bf16[1808,128]{1,0:T(8,128)(2,1)S(1)} %collective-permute-done.other_ref) | copy-start | bytes 1388548

commit v2 on v1

--- a/solution.py
+++ b/solution.py
@@ -38,6 +38,7 @@
         in_specs=[pl.BlockSpec(memory_space=pltpu.SMEM)],
         out_specs=pl.BlockSpec(memory_space=pltpu.VMEM),
         out_shape=jax.ShapeDtypeStruct((owners, 1, LANES), jnp.int32),
+        compiler_params=pltpu.CompilerParams(vmem_limit_bytes=1 << 20),
         name="count_list",
     )(destination)
 
@@ -62,6 +63,7 @@
         ],
         out_specs=pl.BlockSpec(memory_space=pltpu.VMEM),
         out_shape=jax.ShapeDtypeStruct((owners * per_pair,) + rows.shape[1:], rows.dtype),
+        compiler_params=pltpu.CompilerParams(vmem_limit_bytes=4 << 20),
         name="row_copy",
     )(counts, rows)
 
@@ -84,7 +86,7 @@
 
     def body(*refs):
         dest_ref, head_ref, x_ref, w_ref, bias_ref = refs[:5]
-        xt_ref, dact_ref, act_ref = refs[5:8]
+        hidden_ref = refs[5]
         w2_ref = refs[-1]
         step = pl.program_id(0)
 
@@ -95,7 +97,7 @@
                 w2_ref[0, b] = w_ref[3 * b + 1 : 3 * b + 3].reshape(2 * C_OUT, C_IN)
                 w2_ref[1, b, C_OUT:, :] = w_ref[3 * b]
             if lead:
-                places_ref, table_ref = refs[8:10]
+                places_ref, table_ref = refs[6:8]
                 for n in range(own):
                     rank = jnp.int32(0)
                     for k in range(n):
@@ -111,9 +113,7 @@
                 x_ref[pl.ds((m1 + s1) * 25 + (m2 + s2) * 5 + s3, 4)].reshape(4 * own, C_IN)
                 for m2 in range(4)
             ]
-            value = jnp.concatenate(pieces, axis=0)
-            picked.append(value)
-            xt_ref[shift] = value.T
+            picked.append(jnp.concatenate(pieces, axis=0))
         bias_row = jnp.concatenate([bias_ref[...]] * 4, axis=1)
         for p1 in range(2):
             both = jnp.zeros((rows, 2 * LANES), F32)
@@ -133,26 +133,13 @@
                         (((1,), (1,)), ((), ())),
                         preferred_element_type=F32,
                     )
-            hidden = jnp.concatenate([both[:, :LANES], both[:, LANES:] + odd], axis=1) + bias_row
-            gate = jax.nn.sigmoid(hidden)
-            active = hidden * gate
             lanes = slice(p1 * 2 * LANES, (p1 + 1) * 2 * LANES)
-            dact_ref[:, lanes] = gate * (1.0 + hidden * (1.0 - gate))
-            high = active.astype(BF16)
-            act_ref[0, :, lanes] = high
-            act_ref[1, :, lanes] = (active - high.astype(F32)).astype(BF16)
+            total = jnp.concatenate([both[:, :LANES], both[:, LANES:] + odd], axis=1)
+            hidden_ref[:, lanes] = total + bias_row
 
     fixed = lambda *shape: pl.BlockSpec(shape, lambda i: (0,) * len(shape))
-    out_specs = [
-        pl.BlockSpec((8, C_IN, rows), lambda i: (0, 0, i)),
-        pl.BlockSpec((rows, 512), lambda i: (i, 0)),
-        pl.BlockSpec((2, rows, 512), lambda i: (0, i, 0)),
-    ]
-    out_shape = [
-        jax.ShapeDtypeStruct((8, C_IN, count * rows), BF16),
-        jax.ShapeDtypeStruct((count * rows, 512), F32),
-        jax.ShapeDtypeStruct((2, count * rows, 512), BF16),
-    ]
+    out_specs = [pl.BlockSpec((rows, 512), lambda i: (i, 0))]
+    out_shape = [jax.ShapeDtypeStruct((count * rows, 512), F32)]
     if lead:
         out_specs += [pl.BlockSpec(memory_space=pltpu.SMEM), fixed(2, LANES, 512)]
         out_shape += [
@@ -175,6 +162,7 @@
         cost_estimate=pl.CostEstimate(
             flops=count * 2 * rows * C_IN * 3600, transcendentals=0, bytes_accessed=4 << 20
         ),
+        compiler_params=pltpu.CompilerParams(vmem_limit_bytes=16 << 20),
         name="forward_part",
     )(destination, head, patches, weights, bias)
 
@@ -194,32 +182,16 @@
     return rows[0:8] + pltpu.roll(rows[0:8], C_OUT, 1) + rows[8:16]
 
 
-def backward(places, core, arrived, head_table, parts, slots):
-    part_count = len(parts)
-    part_rows = parts[0][1].shape[0]
-    rows = part_count * part_rows
-    steps = part_rows // (16 * slots)
+def backward(places, core, arrived, head_table, cells, hiddens):
+    slots = cells.shape[1]
     span = 16 * slots
+    rows = 4 * span
     groups = C_IN // 32
-
-    def body(*refs):
-        places_ref, core_ref, arrived_ref, head_ref = refs[:4]
-        sources = refs[4 : 4 + 3 * part_count]
-        keep_ref, send_ref, sums_ref = refs[4 + 3 * part_count : 7 + 3 * part_count]
-        xt_ref, dact_ref, act_ref, dsel_ref, grad_ref, pack_ref, sem = refs[7 + 3 * part_count :]
-        copies = []
-        for part in range(part_count):
-            xt_hbm, dact_hbm, act_hbm = sources[3 * part : 3 * part + 3]
-            copies.append(
-                (
-                    pltpu.make_async_copy(dact_hbm, dact_ref.at[part], sem.at[0, part]),
-                    pltpu.make_async_copy(act_hbm, act_ref.at[part], sem.at[1, part]),
-                    pltpu.make_async_copy(xt_hbm, xt_ref.at[part], sem.at[2, part]),
-                )
-            )
-        for kind in range(3):
-            for part in range(part_count):
-                copies[part][kind].start()
+    steps = 4 // len(hiddens)
+
+    def body(places_ref, core_ref, arrived_ref, head_ref, x_ref, *refs):
+        hidden_refs = refs[: len(hiddens)]
+        keep_ref, send_ref, sums_ref, dsel_ref, grad_ref, pack_ref = refs[len(hiddens) :]
         for n in range(slots):
             dsel_ref[:, n, :] = arrived_ref[places_ref[n]].astype(F32)
         fields = dsel_ref[...].reshape(span, LANES).astype(BF16)
@@ -227,31 +199,27 @@
         low_lanes = lane < C_OUT
         bias_sum = jnp.zeros((1, 512), F32)
         head_sum = jnp.zeros((LANES, 512), F32)
-        for part in range(part_count):
-            copies[part][0].wait()
-            copies[part][1].wait()
-            for step in range(steps):
-                m1 = part * steps + step
-                here = slice(step * span, (step + 1) * span)
-                there = slice(m1 * span, (m1 + 1) * span)
-                mine = (lane // 8) % 4 == m1
-                some = jnp.where(mine, fields, jnp.zeros_like(fields))
-                upstream = jnp.dot(some, head_ref[0], preferred_element_type=F32)
-                upstream = upstream + jnp.dot(some, head_ref[1], preferred_element_type=F32)
-                grad = upstream * dact_ref[part, here, :]
-                bias_sum = bias_sum + jnp.sum(grad, axis=0, keepdims=True)
-                grad_ref[there, :] = grad.astype(BF16)
-                blk = [grad[:, b * LANES : (b + 1) * LANES] for b in range(4)]
-                for k, (lo, hi) in enumerate(((0, 2), (1, 3), (2, 3))):
-                    packed = jnp.where(low_lanes, pltpu.roll(blk[lo], C_OUT, 1), blk[hi])
-                    pack_ref[there, k * LANES : (k + 1) * LANES] = packed.astype(BF16)
-                for term in range(2):
-                    head_sum = head_sum + lax.dot_general(
-                        some,
-                        act_ref[part, term, here, :],
-                        (((0,), (0,)), ((), ())),
-                        preferred_element_type=F32,
-                    )
+        for m1 in range(4):
+            here = slice(m1 * span, (m1 + 1) * span)
+            mine = (lane // 8) % 4 == m1
+            some = jnp.where(mine, fields, jnp.zeros_like(fields))
+            upstream = jnp.dot(some, head_ref[0], preferred_element_type=F32)
+            upstream = upstream + jnp.dot(some, head_ref[1], preferred_element_type=F32)
+            hidden = hidden_refs[m1 // steps][(m1 % steps) * span : (m1 % steps + 1) * span, :]
+            gate = jax.nn.sigmoid(hidden)
+            active = hidden * gate
+            grad = upstream * (gate * (1.0 + hidden * (1.0 - gate)))
+            bias_sum = bias_sum + jnp.sum(grad, axis=0, keepdims=True)
+            grad_ref[here, :] = grad.astype(BF16)
+            blk = [grad[:, b * LANES : (b + 1) * LANES] for b in range(4)]
+            for k, (lo, hi) in enumerate(((0, 2), (1, 3), (2, 3))):
+                packed = jnp.where(low_lanes, pltpu.roll(blk[lo], C_OUT, 1), blk[hi])
+                pack_ref[here, k * LANES : (k + 1) * LANES] = packed.astype(BF16)
+            high = active.astype(BF16)
+            for term in (high, (active - high.astype(F32)).astype(BF16)):
+                head_sum = head_sum + lax.dot_general(
+                    some, term, (((0,), (0,)), ((), ())), preferred_element_type=F32
+                )
         row = lax.broadcasted_iota(jnp.int32, (LANES, 512), 0)
         col = lax.broadcasted_iota(jnp.int32, (LANES, 512), 1)
         head_sum = jnp.where(row % 8 == col // C_OUT, head_sum, 0.0)
@@ -264,19 +232,19 @@
         sums_ref[...] = folded
         send_ref[groups * BLOCKS * 16 :, :] = split_sums(folded)
         mine_core = core_ref[0]
-        for part in range(part_count):
-            copies[part][2].wait()
 
         def product(shift, at_ref, lanes):
-            result = None
-            for part in range(part_count):
-                term = jnp.dot(
-                    xt_ref[part, shift],
-                    at_ref[part * part_rows : (part + 1) * part_rows, lanes],
-                    preferred_element_type=F32,
-                )
-                result = term if result is None else result + term
-            return result
+            s1, s2, s3 = shift // 4, (shift // 2) % 2, shift % 2
+            pieces = []
+            for m in range(16):
+                cell = (m // 4 + s1) * 25 + (m % 4 + s2) * 5 + s3
+                pieces.append(x_ref[cell : cell + 4].reshape(4 * slots, C_IN))
+            return lax.dot_general(
+                jnp.concatenate(pieces, axis=0),
+                at_ref[:, lanes],
+                (((0,), (0,)), ((), ())),
+                preferred_element_type=F32,
+            )
 
         def put(block, value):
             split = value.reshape(groups, 2, 16, LANES)
@@ -286,17 +254,16 @@
             for g in range(groups):
                 send_ref[(g * BLOCKS + block) * 16 : (g * BLOCKS + block + 1) * 16, :] = other[g]
 
-        for shift, lo, count, blocks in (
-            (0, 0, 2, (4, 5)),
-            (0, 2, 2, (7, 8)),
-            (4, 2, 2, (1, 2)),
-            (6, 3, 1, (0,)),
-        ):
-            value = product(shift, grad_ref, slice(lo * LANES, (lo + count) * LANES))
-            for k, block in enumerate(blocks):
-                put(block, value[:, k * LANES : (k + 1) * LANES])
-        put(3, product(2, grad_ref, slice(LANES, 2 * LANES)))
-        put(6, product(2, grad_ref, slice(3 * LANES, 4 * LANES)))
+        value = product(0, grad_ref, slice(0, 4 * LANES))
+        for k, block in enumerate((4, 5, 7, 8)):
+            put(block, value[:, k * LANES : (k + 1) * LANES])
+        value = product(4, grad_ref, slice(2 * LANES, 4 * LANES))
+        put(1, value[:, 0:LANES])
+        put(2, value[:, LANES:])
+        put(0, product(6, grad_ref, slice(3 * LANES, 4 * LANES)))
+        value = product(2, grad_ref, slice(LANES, 4 * LANES))
+        put(3, value[:, 0:LANES])
+        put(6, value[:, 2 * LANES :])
         value = product(1, pack_ref, slice(0, 2 * LANES))
         put(9, value[:, 0:LANES])
         put(10, value[:, LANES:])
@@ -306,10 +273,9 @@
 
     smem = pl.BlockSpec(memory_space=pltpu.SMEM)
     vmem = pl.BlockSpec(memory_space=pltpu.VMEM)
-    hbm = pl.BlockSpec(memory_space=pl.ANY)
-    return pl.pallas_call(
-        body,
-        in_specs=[smem, smem, vmem, vmem] + [hbm] * (3 * part_count),
+    return pl.pallas_call(
+        body,
+        in_specs=[smem, smem] + [vmem] * (3 + len(hiddens)),
         out_specs=[vmem, vmem, vmem],
         out_shape=[
             jax.ShapeDtypeStruct((groups, BLOCKS * 16, LANES), F32),
@@ -317,16 +283,13 @@
             jax.ShapeDtypeStruct((8, LANES), F32),
         ],
         scratch_shapes=[
-            pltpu.VMEM((part_count, 8, C_IN, part_rows), BF16),
-            pltpu.VMEM((part_count, part_rows, 512), F32),
-            pltpu.VMEM((part_count, 2, part_rows, 512), BF16),
             pltpu.VMEM((16, slots, LANES), F32),
             pltpu.VMEM((rows, 512), BF16),
             pltpu.VMEM((rows, 3 * LANES), BF16),
-            pltpu.SemaphoreType.DMA((3, part_count)),
         ],
+        compiler_params=pltpu.CompilerParams(vmem_limit_bytes=24 << 20),
         name="backward",
-    )(places, core, arrived, head_table, *[a for part in parts for a in part])
+    )(places, core, arrived, head_table, cells, *hiddens)
 
 
 def pair_sum(keep, sums, other):
@@ -343,6 +306,7 @@
     return pl.pallas_call(
         body,
         out_shape=jax.ShapeDtypeStruct((groups, block_rows + SUM_ROWS, LANES), BF16),
+        compiler_params=pltpu.CompilerParams(vmem_limit_bytes=8 << 20),
         name="pair_sum",
     )(keep, sums, other)
 
@@ -373,6 +337,7 @@
             jax.ShapeDtypeStruct((1, C_OUT), F32),
             jax.ShapeDtypeStruct((FIELDS, C_OUT), F32),
         ],
+        compiler_params=pltpu.CompilerParams(vmem_limit_bytes=4 << 20),
         name="final_sum",
     )(arrived)
 
@@ -410,10 +375,11 @@
         )
         for first in (0, 2)
     ]
-    places, head_table = parts[0][3:]
-    parts = [part[:3] for part in parts]
+    places, head_table = parts[0][1:]
     core = (my_index % 2).astype(jnp.int32).reshape(1)
-    keep, send, sums = backward(places, core, arrived, head_table, parts, own_rows)
+    keep, send, sums = backward(
+        places, core, arrived, head_table, cells, [part[0] for part in parts]
+    )
     other = lax.ppermute(send, "domain", [(i, i ^ 1) for i in range(owners)])
     payload = pair_sum(keep, sums, other)
 

time: 66.2 us -> 52.6 us (0.79)
  Pallas kernels: 23.4 us -> 10.9 us
  blocking collectives: 20 us -> 16.8 us
  waiting for transfers between devices: 5.65 us -> 7.7 us
    pallas_call x2, Pallas kernels: 9.11 us -> 3.79 us  [forward_part(): pl.pallas_call(body, grid=(count,), in_specs=[pl.BlockSpec(memory_space=p...]
    pallas_call x1, Pallas kernels: 7.25 us -> 3.53 us  [backward(): pl.pallas_call(body, in_specs=[smem, smem] + [vmem] * (3 + len(hiddens)),...]
    all_to_all x1, waiting for transfers between devices: 0.01 us -> 3.37 us  [on_device(): lax.all_to_all(outgoing.reshape(owners, per_pair, 16, LANES), 'domain', s...]
    all_to_all x1, blocking collectives: 20 us -> 16.8 us  [on_device(): lax.all_to_all(payload, 'domain', split_axis=0, concat_axis=0, tiled=True...]
    pallas_call x1, Pallas kernels: 2.24 us -> 0.15 us  [pair_sum(): pl.pallas_call(body, out_shape=jax.ShapeDtypeStruct((groups, block_rows +...]
    all_to_all x1, waiting for transfers between devices: 3.88 us -> 2.52 us  [on_device(): lax.all_to_all(count_list(destination, owners), 'domain', split_axis=0, c...]
    transpose x1, local copies, waits for them, and re-layouts: 0.48 us -> 1.66 us  [on_device(): rows = rows.transpose(0, 4, 6, 1, 2, 3, 5, 7).reshape(train_rows, 16, LANES)]
    pallas_call x1, Pallas kernels: 1.85 us -> 0.82 us  [final_sum(): pl.pallas_call(body, out_shape=[jax.ShapeDtypeStruct((TAPS, per_block, C_...]
  transfers between devices with their start and end apart: 3 -> 3, of which waited for: 2 -> 3; matrix products, arithmetic and copies ran while one was open for 4% -> 7% of each run, Pallas kernels for 14% -> 7%
where the time goes in v2:
time: 52.6 us; the launch traced here: 52.3 us
  blocking collectives  16.8 us (32%)
  starting transfers between devices  11 us (21%)
  Pallas kernels  10.9 us (21%)
  waiting for transfers between devices  7.7 us (15%)
  local copies, waits for them, and re-layouts  5.13 us (10%)
  between operations  0.77 us (1%)
    all_to_all x1, blocking collectives, on_device(): lax.all_to_all(payload, 'domain', split_axis=0, concat_axis=0, tiled=True...  16.8 us
    all_to_all x1, starting transfers between devices, on_device(): lax.all_to_all(count_list(destination, owners), 'domain', split_axis=0, c...  7.41 us
    pallas_call x2, Pallas kernels, forward_part(): pl.pallas_call(body, grid=(count,), in_specs=[pl.BlockSpec(memory_space=p...  3.79 us
    pallas_call x1, Pallas kernels, backward(): pl.pallas_call(body, in_specs=[smem, smem] + [vmem] * (3 + len(hiddens)),...  3.53 us
    all_to_all x1, starting transfers between devices, on_device(): lax.all_to_all(outgoing.reshape(owners, per_pair, 16, LANES), 'domain', s...  3.51 us
    all_to_all x1, waiting for transfers between devices, on_device(): lax.all_to_all(outgoing.reshape(owners, per_pair, 16, LANES), 'domain', s...  3.37 us
    unnamed x15, local copies, waits for them, and re-layouts  3.24 us
    all_to_all x1, waiting for transfers between devices, on_device(): lax.all_to_all(count_list(destination, owners), 'domain', split_axis=0, c...  2.52 us
  transfers between devices with their start and end apart: 3, of which 3 were waited for; matrix products, arithmetic and copies ran while one was open for 7% of the time, Pallas kernels for 7%

profile of v2, /device:TPU:0, one launch (start us, length us, event | category | flops | bytes accessed | tf_op | source)
XLA Modules:
  0.0 52.3 jit_solution(1226702644498767071)
XLA Ops:
  0.6 0.0 copy-start.1
  0.6 0.6 %copy-done.1 = s32[16]{0:T(128)S(1)} copy-done((s32[16]{0:T(128)S(1)}, s32[16]{0:T(128)}, u32[]{:S(2)}) %copy-start.1) | copy-done | bytes 88
  1.3 1.2 %count_list.1 = s32[16,1,128]{2,1,0:T(1,128)} custom-call(s32[16]{0:T(128)S(1)} %copy-done.1), custom_call_target="tpu_custom_call" | custom-call | tf_op jit(solution)/shard_map/count_list/pallas_call | solution.py:36
  2.5 7.4 %all-to-all-start = ((s32[16,1,128]{2,1,0:T(1,128)}), s32[16,1,128]{2,1,0:T(1,128)S(1)}, u32[]{:S(2)}, u32[]{:S(2)}) async-start(s32[16,1,128]{2,1,0:T(1,128)} %count_list.1), calls=%async_computation | async-start | bytes 16384 | tf_op jit(solution)/shard_map/all_to_all | solution.py:359
  9.9 1.9 %copy.10 = bf16[32,4,512]{0,2,1:T(8,128)(2,1)} copy(bf16[32,4,512]{2,1,0:T(4,128)(2,1)} %param.8) | data formatting | bytes 262144 | tf_op args[2]
  11.8 1.7 %copy.11 = bf16[32,4,4,4,4,2,2,2]{0,7,6,5,4,3,2,1:T(2,128)(2,1)S(1)} copy(bf16[32,4,4,4,4,2,2,2]{0,7,2,6,1,5,4,3:T(2,128)(2,1)} %bitcast.25) | data formatting | bytes 262144 | tf_op jit(solution)/shard_map/transpose | solution.py:364
  13.5 0.2 copy.12.rows_ref
  13.7 2.5 %all-to-all-done.count_ref = s32[16,1,128]{2,1,0:T(1,128)S(1)} async-done(((s32[16,1,128]{2,1,0:T(1,128)}), s32[16,1,128]{2,1,0:T(1,128)S(1)}, u32[]{:S(2)}, u32[]{:S(2)}) %all-to-all-start) | async-done | bytes 8224 | tf_op jit(solution)/shard_map/all_to_all | solution.py:359
  16.2 1.5 %row_copy.1 = bf16[32,16,128]{2,1,0:T(8,128)(2,1)} custom-call(s32[16,1,128]{2,1,0:T(1,128)S(1)} %all-to-all-done.count_ref, bf16[32,16,128]{2,1,0:T(8,128)(2,1)S(1)} %copy.12.rows_ref), custom_call_target="tpu_custom_call" | custom-call | tf_op jit(solution)/shard_map/row_copy/pallas_call | solution.py:58
  17.7 3.5 %all-to-all-start.1 = ((bf16[16,2,16,128]{3,2,1,0:T(8,128)(2,1)}), bf16[16,2,16,128]{3,2,1,0:T(8,128)(2,1)S(1)}, u32[]{:S(2)}, u32[]{:S(2)}) async-start(bf16[16,2,16,128]{3,2,1,0:T(8,128)(2,1)} %bitcast.8), calls=%async_computation.1 | async-start | bytes 262144 | tf_op jit(solution)/shard_map/all_to_all | solution.py:366
  21.2 0.0 copy-start.5
  21.2 0.0 copy-start.2
  21.3 0.0 copy-start.6
  21.3 0.6 %copy-done.5 = f32[64,4]{0,1:T(4,128)S(1)} copy-done((f32[64,4]{0,1:T(4,128)S(1)}, f32[64,4]{0,1:T(4,128)}, u32[]{:S(2)}) %copy-start.5) | copy-done | bytes 1048
  21.9 1.8 %forward_part.3.refs_1_ = f32[512,512]{1,0:T(8,128)S(1)} custom-call(s32[16]{0:T(128)S(1)} %copy-done.2, f32[4,64]{1,0:T(4,128)S(1)} %bitcast.20, bf16[125,16,256]{2,1,0:T(8,128)(2,1)S(1)} %bitcast.14, bf16[27,64,256]{2,1,0:T(8,128)(2,1)S(1)} %bitcast.18, f32[1,64]{1,0:T(1,128)S(1)} %bitcast.22), custom_call_target="tpu_custom_call" | custom-call | flops 943718400 | bytes 4194304 | tf_op jit(solution)/shard_map/forward_part/pallas_call | solution.py:149
  23.8 0.0 copy-done.4
  23.8 2.0 %forward_part.2 = (f32[512,512]{1,0:T(8,128)S(1)}, s32[16]{0:T(128)S(1)}, bf16[2,128,512]{2,1,0:T(8,128)(2,1)S(1)}) custom-call(s32[16]{0:T(128)S(1)} %copy-done.2, f32[4,64]{1,0:T(4,128)S(1)} %bitcast.21, bf16[125,16,256]{2,1,0:T(8,128)(2,1)S(1)} %bitcast.15, bf16[27,64,256]{2,1,0:T(8,128)(2,1)S(1)} %bitcast.19, f32[1,64]{1,0:T(1,128)S(1)} %bitcast.23), custom_call_target="tpu_custom_call" | custom-call | flops 943718400 | bytes 4194304 | tf_op jit(solution)/shard_map/forward_part/pallas_call | solution.py:149
  25.7 3.4 %all-to-all-done.1 = bf16[16,2,16,128]{3,2,1,0:T(8,128)(2,1)S(1)} async-done(((bf16[16,2,16,128]{3,2,1,0:T(8,128)(2,1)}), bf16[16,2,16,128]{3,2,1,0:T(8,128)(2,1)S(1)}, u32[]{:S(2)}, u32[]{:S(2)}) %all-to-all-start.1) | async-done | bytes 131104 | tf_op jit(solution)/shard_map/all_to_all | solution.py:366
  29.1 3.5 %backward.1 = (f32[8,224,128]{2,1,0:T(8,128)S(1)}, bf16[1808,128]{1,0:T(8,128)(2,1)S(1)}, f32[8,128]{1,0:T(8,128)S(1)}) custom-call(s32[16]{0:T(128)S(1)} %get-tuple-element.12.places_ref, s32[1]{0:T(128)} %bitcast.4.core_ref, bf16[32,16,128]{2,1,0:T(8,128)(2,1)S(1)} %bitcast.17, bf16[2,128,512]{2,1,0:T(8,128)(2,1)S(1)} %get-tuple-element.13.head_ref, ...), custom_call_target="tpu_custom_call" | custom-call | tf_op jit(solution)/shard_map/backward/pallas_call | solution.py:276
  32.6 0.1 collective-permute-start
  32.7 1.8 %collective-permute-done.other_ref = bf16[1808,128]{1,0:T(8,128)(2,1)S(1)} collective-permute-done((bf16[1808,128]{1,0:T(8,128)(2,1)S(1)}, bf16[1808,128]{1,0:T(8,128)(2,1)S(1)}, u32[]{:S(2)}, u32[]{:S(2)}) %collective-permute-start) | collective-permute-done | bytes 462880 | tf_op jit(solution)/shard_map/ppermute | solution.py:383
  34.5 0.1 pair_sum.1
  34.7 16.8 %all_to_all.15.in_ref = bf16[8,240,128]{2,1,0:T(8,128)(2,1)S(1)} all-to-all(bf16[8,240,128]{2,1,0:T(8,128)(2,1)S(1)} %pair_sum.1), channel_id=1, replica_groups={{0,2,4,6,8,10,12,14},{1,3,5,7,9,11,13,15},{16,18,20,22,24,26,28,30},{17..., dimensions={0} | all-to-all | bytes 983040 | tf_op jit(solution)/shard_map/all_to_all | solution.py:395
  51.5 0.8 %final_sum.1 = (f32[27,16,64]{2,1,0:T(8,128)}, f32[1,64]{1,0:T(1,128)}, f32[4,64]{1,0:T(4,128)}) custom-call(bf16[8,240,128]{2,1,0:T(8,128)(2,1)S(1)} %all_to_all.15.in_ref), custom_call_target="tpu_custom_call" | custom-call | tf_op jit(solution)/shard_map/final_sum/pallas_call | solution.py:333
  (7 shorter events, 0.0 us)
Async XLA Ops:
  0.6 0.7 %copy-start.1 = (s32[16]{0:T(128)S(1)}, s32[16]{0:T(128)}, u32[]{:S(2)}) copy-start(s32[16]{0:T(128)} %refs_0_.3) | copy-start | bytes 196
  2.5 13.8 %all-to-all-start = ((s32[16,1,128]{2,1,0:T(1,128)}), s32[16,1,128]{2,1,0:T(1,128)S(1)}, u32[]{:S(2)}, u32[]{:S(2)}) async-start(s32[16,1,128]{2,1,0:T(1,128)} %count_list.1), calls=%async_computation | async-start | bytes 16384 | tf_op jit(solution)/shard_map/all_to_all | solution.py:359
  11.8 9.5 %copy-start = (bf16[16,125,256]{2,0,1:T(8,128)(2,1)S(1)}, bf16[16,125,256]{2,0,1:T(8,128)(2,1)}, u32[]{:S(2)}) copy-start(bf16[16,125,256]{2,0,1:T(8,128)(2,1)} %param.6) | copy-start | bytes 3072004
  11.8 9.5 %copy-start.3 = (bf16[256,27,64]{0,2,1:T(8,128)(2,1)S(1)}, bf16[256,27,64]{0,2,1:T(8,128)(2,1)}, u32[]{:S(2)}) copy-start(bf16[256,27,64]{0,2,1:T(8,128)(2,1)} %param.9) | copy-start | bytes 2654212
  17.7 11.4 %all-to-all-start.1 = ((bf16[16,2,16,128]{3,2,1,0:T(8,128)(2,1)}), bf16[16,2,16,128]{3,2,1,0:T(8,128)(2,1)S(1)}, u32[]{:S(2)}, u32[]{:S(2)}) async-start(bf16[16,2,16,128]{3,2,1,0:T(8,128)(2,1)} %bitcast.8), calls=%async_computation.1 | async-start | bytes 262144 | tf_op jit(solution)/shard_map/all_to_all | solution.py:366
  21.2 0.7 %copy-start.5 = (f32[64,4]{0,1:T(4,128)S(1)}, f32[64,4]{0,1:T(4,128)}, u32[]{:S(2)}) copy-start(f32[64,4]{0,1:T(4,128)} %param.11) | copy-start | bytes 3076
  21.2 0.7 %copy-start.2 = (s32[16]{0:T(128)S(1)}, s32[16]{0:T(128)}, u32[]{:S(2)}) copy-start(s32[16]{0:T(128)} %refs_0_.3) | copy-start | bytes 196
  21.3 0.7 %copy-start.6 = (f32[64]{0:T(128)S(1)}, f32[64]{0:T(128)}, u32[]{:S(2)}) copy-start(f32[64]{0:T(128)} %param.10) | copy-start | bytes 772
  21.9 1.8 %copy-start.4 = (bf16[256,27,64]{0,2,1:T(8,128)(2,1)S(1)}, bf16[256,27,64]{0,2,1:T(8,128)(2,1)}, u32[]{:S(2)}) copy-start(bf16[256,27,64]{0,2,1:T(8,128)(2,1)} %param.9) | copy-start | bytes 2654212
  32.6 1.9 %collective-permute-start = (bf16[1808,128]{1,0:T(8,128)(2,1)S(1)}, bf16[1808,128]{1,0:T(8,128)(2,1)S(1)}, u32[]{:S(2)}, u32[]{:S(2)}) collective-permute-start(bf16[1808,128]{1,0:T(8,128)(2,1)S(1)} %get-tuple-element.17), channel_id=1, source_target_pairs={{0,1},{1,0},{2,3},{3,2},{4,5},{5,4},{6,7},{7,6},{8,9},{9,8},{10,11... | collective-permute-start | bytes 1388552 | tf_op jit(solution)/shard_map/ppermute | solution.py:383

commit v3 on v2

v3 whole, which is shorter than its diff:
```python
import jax
import jax.numpy as jnp
import numpy as np
from jax import lax
from jax.experimental import pallas as pl
from jax.experimental.pallas import tpu as pltpu
from jax.sharding import PartitionSpec as P

C_IN = 256
C_OUT = 64
FIELDS = 4
TAPS = 27
PS = 4
PAD = 5
CELLS = PAD**3
FINE = 512
LANES = 128
BLOCKS = 14
F32 = jnp.float32
BF16 = jnp.bfloat16
HALF_TAPS = [(b * 3 + 1, b * 3 + 2) for b in range(9)]
HALF_TAPS += [(4 * 3, 7 * 3), (5 * 3, 8 * 3), (3 * 3, 6 * 3), (1 * 3, 2 * 3), (None, 0)]


def row_copy(listing, me, rows, per_pair):
    owners, _, own = listing.shape
    lines = owners * per_pair * FIELDS

    def body(me_ref, listing_ref, rows_ref, out_ref):
        hits = (listing_ref[...].reshape(owners, own) == me_ref[0]).astype(F32)
        counts = jnp.broadcast_to(jnp.sum(hits, axis=1, keepdims=True), (owners, LANES)).astype(BF16)
        line = lax.broadcasted_iota(jnp.int32, (lines, owners), 0)
        owner = lax.broadcasted_iota(jnp.int32, (lines, owners), 1)
        before = (owner < line // (per_pair * FIELDS)).astype(F32).astype(BF16)
        starts = jnp.dot(before, counts, preferred_element_type=F32)
        line = lax.broadcasted_iota(jnp.int32, (lines, LANES), 0)
        lane = lax.broadcasted_iota(jnp.int32, (lines, LANES), 1)
        wanted = starts.astype(jnp.int32) * FIELDS + line % (per_pair * FIELDS)
        pick = (wanted == lane).astype(F32).astype(BF16)
        out_ref[...] = jnp.dot(pick, rows_ref[...], preferred_element_type=F32).astype(BF16)

    vmem = pl.BlockSpec(memory_space=pltpu.VMEM)
    return pl.pallas_call(
        body,
        in_specs=[pl.BlockSpec(memory_space=pltpu.SMEM), vmem, vmem],
        out_specs=vmem,
        out_shape=jax.ShapeDtypeStruct((lines, FINE), BF16),
        compiler_params=pltpu.CompilerParams(vmem_limit_bytes=4 << 20),
        cost_estimate=pl.CostEstimate(flops=8 << 30, transcendentals=0, bytes_accessed=1 << 20),
        name="row_copy",
    )(me, listing, rows)


def spread(destination, owners):
    own = destination.shape[0]

    def body(in_ref, out_ref):
        out_ref[...] = jnp.broadcast_to(in_ref[...].reshape(1, 1, own), (owners, 1, own))

    return pl.pallas_call(
        body, out_shape=jax.ShapeDtypeStruct((owners, 1, own), jnp.int32), name="spread"
    )(destination.reshape(1, own))


def turn_terms():
    fine = lax.broadcasted_iota(jnp.int32, (LANES, LANES), 0)
    lane = lax.broadcasted_iota(jnp.int32, (LANES, LANES), 1)
    to = ((fine >> 4) & 3) * 32 + (fine >> 6) * 16 + (fine & 15)
    return (to == lane).astype(F32).astype(BF16)


def head_terms(head):
    rows = jnp.concatenate([jnp.broadcast_to(head[f : f + 1], (32, C_OUT)) for f in range(FIELDS)], axis=0)
    pair = jnp.concatenate([rows, rows], axis=1)
    table = jnp.concatenate([pair] * 4, axis=1)
    row = lax.broadcasted_iota(jnp.int32, table.shape, 0)
    col = lax.broadcasted_iota(jnp.int32, table.shape, 1)
    table = jnp.where((row // 8 % 4) * 2 + row % 2 == col // C_OUT, table, 0.0)
    high = table.astype(BF16)
    return jnp.concatenate([high, (table - high.astype(F32)).astype(BF16)], axis=0)


def forward_part(patches, first, count, weights, bias, destination, head, slots, per_pair):
    own = patches.shape[1]
    rows = 16 * own
    lead = first == 0

    def body(*refs):
        dest_ref, head_ref, x_ref, w_ref, bias_ref = refs[:5]
        hidden_ref = refs[5]
        w2_ref = refs[-1]
        step = pl.program_id(0)

        @pl.when(step == 0)
        def _():
            w2_ref[1, :, 0:C_OUT, :] = jnp.zeros((9, C_OUT, C_IN), BF16)
            for b in range(9):
                w2_ref[0, b] = w_ref[3 * b + 1 : 3 * b + 3].reshape(2 * C_OUT, C_IN)
                w2_ref[1, b, C_OUT:, :] = w_ref[3 * b]
            if lead:
                pick_ref, table_ref = refs[6:8]
                line = lax.broadcasted_iota(jnp.int32, (FIELDS * own, slots * FIELDS), 0)
                lane = lax.broadcasted_iota(jnp.int32, (FIELDS * own, slots * FIELDS), 1)
                wanted = jnp.zeros_like(line)
                for n in range(own):
                    rank = jnp.int32(0)
                    for k in range(n):
                        rank = rank + (dest_ref[k] == dest_ref[n]).astype(jnp.int32)
                    wanted = jnp.where(line % own == n, dest_ref[n] * per_pair + rank, wanted)
                wanted = wanted * FIELDS + line // own
                pick_ref[...] = (wanted == lane).astype(F32).astype(BF16)
                table_ref[...] = head_terms(head_ref[...])

        m1 = step + first
        picked = []
        for shift in range(8):
            s1, s2, s3 = shift // 4, (shift // 2) % 2, shift % 2
            pieces = [
                x_ref[pl.ds((m1 + s1) * 25 + (m2 + s2) * 5 + s3, 4)].reshape(4 * own, C_IN)
                for m2 in range(4)
            ]
            picked.append(jnp.concatenate(pieces, axis=0))
        bias_row = jnp.concatenate([bias_ref[...]] * 4, axis=1)
        for p1 in range(2):
            both = jnp.zeros((rows, 2 * LANES), F32)
            odd = jnp.zeros((rows, LANES), F32)
            for s1 in range(p1 + 1):
                k1 = 1 if p1 == 0 else (2 if s1 == 0 else 0)
                for s3 in range(2):
                    both = both + lax.dot_general(
                        picked[s1 * 4 + s3],
                        w2_ref[s3, k1 * 3 + 1 : k1 * 3 + 3].reshape(2 * LANES, C_IN),
                        (((1,), (1,)), ((), ())),
                        preferred_element_type=F32,
                    )
                    odd = odd + lax.dot_general(
                        picked[s1 * 4 + 2 + s3],
                        w2_ref[s3, k1 * 3],
                        (((1,), (1,)), ((), ())),
                        preferred_element_type=F32,
                    )
            lanes = slice(p1 * 2 * LANES, (p1 + 1) * 2 * LANES)
            total = jnp.concatenate([both[:, :LANES], both[:, LANES:] + odd], axis=1)
            hidden_ref[:, lanes] = total + bias_row

    fixed = lambda *shape: pl.BlockSpec(shape, lambda i: (0,) * len(shape))
    out_specs = [pl.BlockSpec((rows, 512), lambda i: (i, 0))]
    out_shape = [jax.ShapeDtypeStruct((count * rows, 512), F32)]
    if lead:
        out_specs += [fixed(FIELDS * own, slots * FIELDS), fixed(2 * LANES, 512)]
        out_shape += [
            jax.ShapeDtypeStruct((FIELDS * own, slots * FIELDS), BF16),
            jax.ShapeDtypeStruct((2 * LANES, 512), BF16),
        ]
    return pl.pallas_call(
        body,
        grid=(count,),
        in_specs=[
            pl.BlockSpec(memory_space=pltpu.SMEM),
            fixed(FIELDS, C_OUT),
            fixed(CELLS, own, C_IN),
            fixed(TAPS, C_OUT, C_IN),
            fixed(1, C_OUT),
        ],
        out_specs=out_specs,
        out_shape=out_shape,
        scratch_shapes=[pltpu.VMEM((2, 9, LANES, C_IN), BF16)],
        cost_estimate=pl.CostEstimate(
            flops=count * 2 * rows * C_IN * 3600, transcendentals=0, bytes_accessed=4 << 20
        ),
        compiler_params=pltpu.CompilerParams(vmem_limit_bytes=16 << 20),
        name="forward_part",
    )(destination, head, patches, weights, bias)


def split_sums(sums):
    high = sums.astype(BF16).astype(F32)
    return jnp.concatenate([high, sums - high], axis=0)


def backward(core, pick, arrived, head_table, cells, hidden):
    slots = cells.shape[1]
    span = 16 * slots
    rows = 4 * span
    groups = C_IN // 32

    def body(
        core_ref, pick_ref, arrived_ref, head_ref, x_ref, hidden_ref, keep_ref, send_ref, grad_ref, pack_ref
    ):
        lane = lax.broadcasted_iota(jnp.int32, (1, LANES), 1)
        chosen = jnp.dot(pick_ref[...], arrived_ref[...], preferred_element_type=F32).astype(BF16)
        turn = turn_terms()
        turned = [
            jnp.dot(chosen[:, m1 * LANES : (m1 + 1) * LANES], turn, preferred_element_type=F32)
            for m1 in range(4)
        ]
        pieces = []
        for j in range(16):
            piece = jnp.zeros((slots, LANES), F32)
            for f in range(FIELDS):
                part = turned[j // 4][f * slots : (f + 1) * slots]
                shift = (f - j % 4) * 32 % LANES
                part = pltpu.roll(part, shift, 1) if shift else part
                piece = jnp.where(lane // 32 == f, part, piece)
            pieces.append(piece.astype(BF16))
        fields = jnp.concatenate(pieces, axis=0)
        low_lanes = lane < C_OUT
        bias_sum = jnp.zeros((1, 512), F32)
        head_sum = jnp.zeros((LANES, 512), F32)
        for m3 in range(4):
            here = [slice((j * 4 + m3) * slots, (j * 4 + m3 + 1) * slots) for j in range(16)]
            mine = (lane // 2) % 4 == m3
            some = jnp.where(mine, fields, jnp.zeros_like(fields))
            upstream = jnp.dot(
                jnp.concatenate([some, some], axis=1), head_ref[...], preferred_element_type=F32
            )
            hidden = jnp.concatenate([hidden_ref[rows_of, :] for rows_of in here], axis=0)
            gate = jax.nn.sigmoid(hidden)
            active = hidden * gate
            grad = upstream * (gate * (1.0 + hidden * (1.0 - gate)))
            bias_sum = bias_sum + jnp.sum(grad, axis=0, keepdims=True)
            low = grad.astype(BF16)
            for j, rows_of in enumerate(here):
                grad_ref[rows_of, :] = low[j * slots : (j + 1) * slots]
            blk = [grad[:, b * LANES : (b + 1) * LANES] for b in range(4)]
            for k, (lo, hi) in enumerate(((0, 2), (1, 3), (2, 3))):
                packed = jnp.where(low_lanes, pltpu.roll(blk[lo], C_OUT, 1), blk[hi])
                packed = packed.astype(BF16)
                for j, rows_of in enumerate(here):
                    pack_ref[rows_of, k * LANES : (k + 1) * LANES] = packed[j * slots : (j + 1) * slots]
            high = active.astype(BF16)
            for term in (high, (active - high.astype(F32)).astype(BF16)):
                head_sum = head_sum + lax.dot_general(
                    some, term, (((0,), (0,)), ((), ())), preferred_element_type=F32
                )
        row = lax.broadcasted_iota(jnp.int32, (LANES, 512), 0)
        col = lax.broadcasted_iota(jnp.int32, (LANES, 512), 1)
        head_sum = jnp.where((row // 8 % 4) * 2 + row % 2 == col // C_OUT, head_sum, 0.0)
        heads = [
            jnp.sum(head_sum[f * 32 : (f + 1) * 32], axis=0, keepdims=True) for f in range(FIELDS)
        ]
        stacked = jnp.concatenate([bias_sum] + heads + [jnp.zeros((3, 512), F32)], axis=0)
        folded = sum(stacked[:, b * LANES : (b + 1) * LANES] for b in range(4))
        folded = folded + pltpu.roll(folded, C_OUT, 1)
        tail = split_sums(folded)
        mine_core = core_ref[0]

        def product(shift, at_ref, lanes):
            s1, s2, s3 = shift // 4, (shift // 2) % 2, shift % 2
            pieces = []
            for m in range(16):
                cell = (m // 4 + s1) * 25 + (m % 4 + s2) * 5 + s3
                pieces.append(x_ref[cell : cell + 4].reshape(4 * slots, C_IN))
            return lax.dot_general(
                jnp.concatenate(pieces, axis=0),
                at_ref[:, lanes],
                (((0,), (0,)), ((), ())),
                preferred_element_type=F32,
            )

        def put(block, value):
            split = value.reshape(groups, 2, 16, LANES)
            even, odd = split[:, 0], split[:, 1]
            if block == BLOCKS - 1:
                even, odd = (jnp.where(low_lanes[None], tail[None], half) for half in (even, odd))
            keep_ref[:, block * 16 : (block + 1) * 16, :] = jnp.where(mine_core == 0, even, odd)
            other = jnp.where(mine_core == 0, odd, even).astype(BF16)
            for g in range(groups):
                send_ref[(g * BLOCKS + block) * 16 : (g * BLOCKS + block + 1) * 16, :] = other[g]

        value = product(0, grad_ref, slice(0, 4 * LANES))
        for k, block in enumerate((4, 5, 7, 8)):
            put(block, value[:, k * LANES : (k + 1) * LANES])
        value = product(4, grad_ref, slice(2 * LANES, 4 * LANES))
        put(1, value[:, 0:LANES])
        put(2, value[:, LANES:])
        put(0, product(6, grad_ref, slice(3 * LANES, 4 * LANES)))
        value = product(2, grad_ref, slice(LANES, 4 * LANES))
        put(3, value[:, 0:LANES])
        put(6, value[:, 2 * LANES :])
        value = product(1, pack_ref, slice(0, 2 * LANES))
        put(9, value[:, 0:LANES])
        put(10, value[:, LANES:])
        put(11, product(3, pack_ref, slice(LANES, 2 * LANES)))
        put(12, product(5, pack_ref, slice(2 * LANES, 3 * LANES)))
        put(13, product(7, pack_ref, slice(LANES, 2 * LANES)))

    smem = pl.BlockSpec(memory_space=pltpu.SMEM)
    vmem = pl.BlockSpec(memory_space=pltpu.VMEM)
    return pl.pallas_call(
        body,
        in_specs=[smem] + [vmem] * 5,
        out_specs=[vmem, vmem],
        out_shape=[
            jax.ShapeDtypeStruct((groups, BLOCKS * 16, LANES), F32),
            jax.ShapeDtypeStruct((groups * BLOCKS * 16, LANES), BF16),
        ],
        scratch_shapes=[
            pltpu.VMEM((rows, 512), BF16),
            pltpu.VMEM((rows, 3 * LANES), BF16),
        ],
        compiler_params=pltpu.CompilerParams(vmem_limit_bytes=24 << 20),
        name="backward",
    )(core, pick, arrived, head_table, cells, hidden)


def pair_sum(keep, other):
    groups, block_rows, _ = keep.shape
    last = block_rows - 16

    def body(keep_ref, other_ref, out_ref):
        low_lanes = lax.broadcasted_iota(jnp.int32, (16, LANES), 1) < C_OUT
        for g in range(groups):
            partner = other_ref[g * block_rows : (g + 1) * block_rows, :].astype(F32)
            total = keep_ref[g] + partner
            out_ref[g, 0:last, :] = total[0:last].astype(BF16)
            tail = total[last:]
            tail = jnp.where(low_lanes, split_sums(tail[0:8] + tail[8:16]), tail)
            out_ref[g, last:, :] = tail.astype(BF16)

    return pl.pallas_call(
        body,
        out_shape=jax.ShapeDtypeStruct((groups, block_rows, LANES), BF16),
        compiler_params=pltpu.CompilerParams(vmem_limit_bytes=8 << 20),
        name="pair_sum",
    )(keep, other)


def final_sum(arrived, scale, per_block):
    sources = arrived.shape[0]

    def body(in_ref, conv_ref, bias_ref, head_ref):
        total = in_ref[0].astype(F32)
        for source in range(1, sources):
            total = total + in_ref[source].astype(F32)
        total = total * scale
        for block, taps in enumerate(HALF_TAPS):
            value = total[block * per_block : (block + 1) * per_block]
            for half, tap in enumerate(taps):
                if tap is not None:
                    conv_ref[tap] = value[:, half * C_OUT : (half + 1) * C_OUT]
        joined = value[0:8] + value[8:16]
        bias_ref[...] = joined[0:1, 0:C_OUT]
        head_ref[...] = joined[1 : 1 + FIELDS, 0:C_OUT]

    return pl.pallas_call(
        body,
        out_shape=[
            jax.ShapeDtypeStruct((TAPS, per_block, C_OUT), F32),
            jax.ShapeDtypeStruct((1, C_OUT), F32),
            jax.ShapeDtypeStruct((FIELDS, C_OUT), F32),
        ],
        compiler_params=pltpu.CompilerParams(vmem_limit_bytes=4 << 20),
        name="final_sum",
    )(arrived)


def on_device(patches, destination, cotangent, conv_weight, conv_bias, head_weight):
    owners = lax.axis_size("domain")
    my_index = lax.axis_index("domain")
    own_rows = patches.shape[0]
    train_rows = cotangent.shape[0]
    per_pair = (train_rows + owners - 1) // owners
    channels = C_IN // owners
    splits = 16 // channels
    if splits > 1:
        order = np.arange(C_IN).reshape(C_IN // 32, splits, 2, channels)
        order = order.transpose(0, 2, 1, 3).reshape(-1)
        patches = patches[:, :, order]
        conv_weight = conv_weight[order]

    listing = lax.all_to_all(
        spread(destination, owners),
        "domain",
        split_axis=0,
        concat_axis=0,
        tiled=True,
    )
    cells = patches.transpose(1, 0, 2)
    weights = conv_weight.transpose(1, 2, 0)
    slots = owners * per_pair
    bias = conv_bias.reshape(1, C_OUT)
    hidden, pick, head_table = forward_part(
        cells, 0, 4, weights, bias, destination, head_weight.T, slots, per_pair
    )
    me = my_index.astype(jnp.int32).reshape(1)
    rows = cotangent.reshape(train_rows * FIELDS, FINE)
    outgoing = row_copy(listing, me, rows, per_pair)
    arrived = lax.all_to_all(
        outgoing.reshape(owners, per_pair * FIELDS, FINE), "domain", split_axis=0, concat_axis=0, tiled=True
    ).reshape(owners * per_pair * FIELDS, FINE)

    core = (my_index % 2).astype(jnp.int32).reshape(1)
    keep, send = backward(core, pick, arrived, head_table, cells, hidden)
    other = lax.ppermute(send, "domain", [(i, i ^ 1) for i in range(owners)])
    payload = pair_sum(keep, other)

    scale = float((owners * own_rows * PS**3) ** (-0.5))
    mates = owners // 2
    groups = [[core_id + 2 * k for k in range(mates)] for core_id in range(2)]
    block_rows = BLOCKS * 16
    if splits > 1:
        tail = jnp.repeat(payload[:, block_rows - 16 :], splits, axis=0)
        blocks = payload.reshape(C_IN // 32, BLOCKS, splits, channels, LANES)
        blocks = blocks.transpose(0, 2, 1, 3, 4).reshape(mates, BLOCKS * channels, LANES)
        payload = jnp.concatenate([blocks, tail], axis=1)
    swapped = lax.all_to_all(
        payload, "domain", split_axis=0, concat_axis=0, tiled=True, axis_index_groups=groups
    )
    if splits > 1:
        tail = jnp.sum(swapped[:, BLOCKS * channels :].astype(F32), axis=0) * scale
        tail = tail[0:8, 0:C_OUT] + tail[8:, 0:C_OUT]
        total = jnp.sum(swapped[:, : BLOCKS * channels].astype(F32), axis=0) * scale
        total = total.reshape(BLOCKS, channels, 2, C_OUT)
        where = {tap: (b, h) for b, pair in enumerate(HALF_TAPS) for h, tap in enumerate(pair)}
        conv = jnp.stack([total[where[t][0], :, where[t][1]] for t in range(TAPS)], axis=1)
        return conv, tail[0], tail[1 : 1 + FIELDS].T
    conv, bias_out, head_out = final_sum(swapped, scale, channels)
    return conv.transpose(1, 0, 2), bias_out.reshape(C_OUT), head_out.T


def solution(mesh):
    placed = (
        P(("groups", "domain"), None, None),
        P(("groups", "domain")),
        P(("groups", "domain"), None, None),
        P(),
        P(),
        P(),
    )
    return jax.shard_map(
        on_device,
        mesh=mesh,
        in_specs=placed,
        out_specs=(P(("groups", "domain"), None, None), P("groups"), P("groups", None)),
        check_vma=False,
    )
```

time: 52.6 us -> 50.7 us (0.964)
  local copies, waits for them, and re-layouts: 5.13 us -> 2.12 us
  waiting for transfers between devices: 7.7 us -> 10.7 us
  Pallas kernels: 10.9 us -> 9.6 us
  blocking collectives: 16.8 us -> 16.2 us
    all_to_all x2, waiting for transfers between devices: 5.89 us -> 8.92 us  [the longest x1 5.41 us: on_device(): lax.all_to_all(spread(destination, owners), 'domain', split_axis=0, conca...]
    unnamed x15 -> x10, local copies, waits for them, and re-layouts: 3.24 us -> 1.18 us
    transpose x1 -> x0, local copies, waits for them, and re-layouts: 1.66 us -> none  [on_device(): rows = rows.transpose(0, 4, 6, 1, 2, 3, 5, 7).reshape(train_rows, 16, LANES)]
    reshape x1, local copies, waits for them, and re-layouts: 0.23 us -> 0.94 us  [on_device(): rows = cotangent.reshape(train_rows * FIELDS, FINE)]
    pallas_call x4, Pallas kernels: 6.31 us -> 5.64 us  [the longest x1 3.24 us: backward(): pl.pallas_call(body, in_specs=[smem] + [vmem] * 5, out_specs=[vmem, vmem]...]
    pallas_call x2 -> x1, Pallas kernels: 3.79 us -> 3.13 us  [forward_part(): pl.pallas_call(body, grid=(count,), in_specs=[pl.BlockSpec(memory_space=p...]
    all_to_all x1, blocking collectives: 16.8 us -> 16.2 us  [on_device(): lax.all_to_all(payload, 'domain', split_axis=0, concat_axis=0, tiled=True...]
  transfers between devices with their start and end apart: 3 -> 3, of which waited for: 3 -> 3; matrix products, arithmetic and copies ran while one was open for 7% -> 2% of each run, Pallas kernels for 7% -> 6%
where the time goes in v3:
time: 50.7 us; the launch traced here: 50.3 us
  blocking collectives  16.2 us (32%)
  starting transfers between devices  11 us (22%)
  waiting for transfers between devices  10.7 us (21%)
  Pallas kernels  9.6 us (19%)
  local copies, waits for them, and re-layouts  2.12 us (4%)
  between operations  0.73 us (1%)
    all_to_all x1, blocking collectives, on_device(): lax.all_to_all(payload, 'domain', split_axis=0, concat_axis=0, tiled=True...  16.2 us
    all_to_all x1, starting transfers between devices, on_device(): lax.all_to_all(spread(destination, owners), 'domain', split_axis=0, conca...  7.41 us
    all_to_all x1, waiting for transfers between devices, on_device(): lax.all_to_all(spread(destination, owners), 'domain', split_axis=0, conca...  5.41 us
    all_to_all x1, starting transfers between devices, on_device(): lax.all_to_all(outgoing.reshape(owners, per_pair * FIELDS, FINE), 'domain...  3.51 us
    all_to_all x1, waiting for transfers between devices, on_device(): lax.all_to_all(outgoing.reshape(owners, per_pair * FIELDS, FINE), 'domain...  3.51 us
    pallas_call x1, Pallas kernels, backward(): pl.pallas_call(body, in_specs=[smem] + [vmem] * 5, out_specs=[vmem, vmem]...  3.24 us
    pallas_call x1, Pallas kernels, forward_part(): pl.pallas_call(body, grid=(count,), in_specs=[pl.BlockSpec(memory_space=p...  3.13 us
    ppermute x1, waiting for transfers between devices, on_device(): other = lax.ppermute(send, 'domain', [(i, i ^ 1) for i in range(owners)])  1.8 us
  transfers between devices with their start and end apart: 3, of which 3 were waited for; matrix products, arithmetic and copies ran while one was open for 2% of the time, Pallas kernels for 6%

profile of v3, /device:TPU:0, one launch (start us, length us, event | category | flops | bytes accessed | tf_op | source)
XLA Modules:
  0.0 50.3 jit_solution(10850648268266087955)
XLA Ops:
  0.6 1.3 %spread.1 = s32[16,1,16]{2,1,0:T(1,128)} custom-call(s32[1,16]{1,0:T(1,128)} %bitcast.15), custom_call_target="tpu_custom_call" | custom-call | tf_op jit(solution)/shard_map/spread/pallas_call | solution.py:60
  1.9 7.4 %all-to-all-start = ((s32[16,1,16]{2,1,0:T(1,128)}), s32[16,1,16]{2,1,0:T(1,128)S(1)}, u32[]{:S(2)}, u32[]{:S(2)}) async-start(s32[16,1,16]{2,1,0:T(1,128)} %spread.1), calls=%async_computation | async-start | bytes 16384 | tf_op jit(solution)/shard_map/all_to_all | solution.py:372
  9.3 0.9 %reshape.34.rows_ref = bf16[128,512]{1,0:T(8,128)(2,1)S(1)} reshape(bf16[32,4,512]{2,1,0:T(4,128)(2,1)} %param.8) | data formatting | bytes 262144 | tf_op jit(solution)/shard_map/reshape | solution.py:387
  10.3 5.4 %all-to-all-done.listing_ref = s32[16,1,16]{2,1,0:T(1,128)S(1)} async-done(((s32[16,1,16]{2,1,0:T(1,128)}), s32[16,1,16]{2,1,0:T(1,128)S(1)}, u32[]{:S(2)}, u32[]{:S(2)}) %all-to-all-start) | async-done | bytes 1056 | tf_op jit(solution)/shard_map/all_to_all | solution.py:372
  15.7 0.0 copy-start
  15.7 0.0 copy-start.1
  15.7 0.0 copy-start.3
  15.7 0.0 copy-start.4
  15.7 1.0 %row_copy.1 = bf16[128,512]{1,0:T(8,128)(2,1)} custom-call(s32[1]{0:T(128)} %bitcast.5.me_ref, s32[16,1,16]{2,1,0:T(1,128)S(1)} %all-to-all-done.listing_ref, bf16[128,512]{1,0:T(8,128)(2,1)S(1)} %reshape.34.rows_ref), custom_call_target="tpu_custom_call" | custom-call | flops 8589934592 | bytes 1048576 | tf_op jit(solution)/shard_map/row_copy/pallas_call | solution.py:43
  16.7 3.5 %all-to-all-start.1 = ((bf16[16,8,512]{2,1,0:T(8,128)(2,1)}), bf16[16,8,512]{2,1,0:T(8,128)(2,1)S(1)}, u32[]{:S(2)}, u32[]{:S(2)}) async-start(bf16[16,8,512]{2,1,0:T(8,128)(2,1)} %bitcast.7), calls=%async_computation.1 | async-start | bytes 262144 | tf_op jit(solution)/shard_map/all_to_all | solution.py:389
  20.2 0.0 copy-done
  20.2 0.0 copy-done.1
  20.3 0.0 copy-done.3
  20.3 0.0 copy-done.4
  20.3 0.0 copy-start.2
  20.3 1.2 %copy-done.2 = bf16[256,27,64]{0,2,1:T(8,128)(2,1)S(1)} copy-done((bf16[256,27,64]{0,2,1:T(8,128)(2,1)S(1)}, bf16[256,27,64]{0,2,1:T(8,128)(2,1)}, u32[]{:S(2)}) %copy-start.2) | copy-done | bytes 884760
  21.4 3.1 %forward_part.1 = (f32[1024,512]{1,0:T(8,128)S(1)}, bf16[64,128]{1,0:T(8,128)(2,1)S(1)}, bf16[256,512]{1,0:T(8,128)(2,1)S(1)}) custom-call(s32[16]{0:T(128)S(1)} %copy-done.1, f32[4,64]{1,0:T(4,128)S(1)} %bitcast.17, bf16[125,16,256]{2,1,0:T(8,128)(2,1)S(1)} %bitcast.12, bf16[27,64,256]{2,1,0:T(8,128)(2,1)S(1)} %bitcast.16, f32[1,64]{1,0:T(1,128)S(1)} %bitcast.18), custom_call_target="tpu_custom_call" | custom-call | flops 1887436800 | bytes 4194304 | tf_op jit(solution)/shard_map/forward_part/pallas_call | solution.py:155
  24.6 3.5 %all-to-all-done.1 = bf16[16,8,512]{2,1,0:T(8,128)(2,1)S(1)} async-done(((bf16[16,8,512]{2,1,0:T(8,128)(2,1)}), bf16[16,8,512]{2,1,0:T(8,128)(2,1)S(1)}, u32[]{:S(2)}, u32[]{:S(2)}) %all-to-all-start.1) | async-done | bytes 131104 | tf_op jit(solution)/shard_map/all_to_all | solution.py:389
  28.1 3.2 %backward.1 = (f32[8,224,128]{2,1,0:T(8,128)S(1)}, bf16[1792,128]{1,0:T(8,128)(2,1)S(1)}) custom-call(s32[1]{0:T(128)} %bitcast.core_ref, bf16[64,128]{1,0:T(8,128)(2,1)S(1)} %get-tuple-element.11.pick_ref, bf16[128,512]{1,0:T(8,128)(2,1)S(1)} %bitcast.14, bf16[256,512]{1,0:T(8,128)(2,1)S(1)} %get-tuple-element.12.head_ref, ...), custom_call_target="tpu_custom_call" | custom-call | tf_op jit(solution)/shard_map/backward/pallas_call | solution.py:290
  31.4 0.1 collective-permute-start
  31.4 1.8 %collective-permute-done.other_ref = bf16[1792,128]{1,0:T(8,128)(2,1)S(1)} collective-permute-done((bf16[1792,128]{1,0:T(8,128)(2,1)S(1)}, bf16[1792,128]{1,0:T(8,128)(2,1)S(1)}, u32[]{:S(2)}, u32[]{:S(2)}) %collective-permute-start) | collective-permute-done | bytes 458784 | tf_op jit(solution)/shard_map/ppermute | solution.py:395
  33.2 0.1 pair_sum.1
  33.3 16.2 %all_to_all.15.in_ref = bf16[8,224,128]{2,1,0:T(8,128)(2,1)S(1)} all-to-all(bf16[8,224,128]{2,1,0:T(8,128)(2,1)S(1)} %pair_sum.1), channel_id=1, replica_groups={{0,2,4,6,8,10,12,14},{1,3,5,7,9,11,13,15},{16,18,20,22,24,26,28,30},{17..., dimensions={0} | all-to-all | bytes 917504 | tf_op jit(solution)/shard_map/all_to_all | solution.py:407
  49.5 0.8 %final_sum.1 = (f32[27,16,64]{2,1,0:T(8,128)}, f32[1,64]{1,0:T(1,128)}, f32[4,64]{1,0:T(4,128)}) custom-call(bf16[8,224,128]{2,1,0:T(8,128)(2,1)S(1)} %all_to_all.15.in_ref), custom_call_target="tpu_custom_call" | custom-call | tf_op jit(solution)/shard_map/final_sum/pallas_call | solution.py:346
Async XLA Ops:
  1.9 13.8 %all-to-all-start = ((s32[16,1,16]{2,1,0:T(1,128)}), s32[16,1,16]{2,1,0:T(1,128)S(1)}, u32[]{:S(2)}, u32[]{:S(2)}) async-start(s32[16,1,16]{2,1,0:T(1,128)} %spread.1), calls=%async_computation | async-start | bytes 16384 | tf_op jit(solution)/shard_map/all_to_all | solution.py:372
  15.7 4.6 %copy-start = (bf16[16,125,256]{2,0,1:T(8,128)(2,1)S(1)}, bf16[16,125,256]{2,0,1:T(8,128)(2,1)}, u32[]{:S(2)}) copy-start(bf16[16,125,256]{2,0,1:T(8,128)(2,1)} %param.6) | copy-start | bytes 3072004
  15.7 4.6 %copy-start.1 = (s32[16]{0:T(128)S(1)}, s32[16]{0:T(128)}, u32[]{:S(2)}) copy-start(s32[16]{0:T(128)} %refs_0_.1) | copy-start | bytes 196
  15.7 4.6 %copy-start.3 = (f32[64,4]{0,1:T(4,128)S(1)}, f32[64,4]{0,1:T(4,128)}, u32[]{:S(2)}) copy-start(f32[64,4]{0,1:T(4,128)} %param.11) | copy-start | bytes 3076
  15.7 4.6 %copy-start.4 = (f32[64]{0:T(128)S(1)}, f32[64]{0:T(128)}, u32[]{:S(2)}) copy-start(f32[64]{0:T(128)} %param.10) | copy-start | bytes 772
  16.7 11.4 %all-to-all-start.1 = ((bf16[16,8,512]{2,1,0:T(8,128)(2,1)}), bf16[16,8,512]{2,1,0:T(8,128)(2,1)S(1)}, u32[]{:S(2)}, u32[]{:S(2)}) async-start(bf16[16,8,512]{2,1,0:T(8,128)(2,1)} %bitcast.7), calls=%async_computation.1 | async-start | bytes 262144 | tf_op jit(solution)/shard_map/all_to_all | solution.py:389
  20.3 1.2 %copy-start.2 = (bf16[256,27,64]{0,2,1:T(8,128)(2,1)S(1)}, bf16[256,27,64]{0,2,1:T(8,128)(2,1)}, u32[]{:S(2)}) copy-start(bf16[256,27,64]{0,2,1:T(8,128)(2,1)} %param.9) | copy-start | bytes 2654212
  31.4 1.9 %collective-permute-start = (bf16[1792,128]{1,0:T(8,128)(2,1)S(1)}, bf16[1792,128]{1,0:T(8,128)(2,1)S(1)}, u32[]{:S(2)}, u32[]{:S(2)}) collective-permute-start(bf16[1792,128]{1,0:T(8,128)(2,1)S(1)} %get-tuple-element.15), channel_id=1, source_target_pairs={{0,1},{1,0},{2,3},{3,2},{4,5},{5,4},{6,7},{7,6},{8,9},{9,8},{10,11... | collective-permute-start | bytes 1376264 | tf_op jit(solution)/shard_map/ppermute | solution.py:395
